TPU v7x, 1024 devices: a whole 8x8x8 slice. The times are simulated.
1024 devices in a mesh: section: 32 (over y, z_lo), ctx: 4 (over z_hi, core), dp: 8 (over x).
Axes of the slice: x: 8, y: 8, z: 8 (z_hi: 2, z_lo: 4; z = z_hi * 4 + z_lo), core: 2. Of those that a mesh axis runs over, the one named last changes fastest.
Arguments:
- q_in: bfloat16 [8, 32, 512, 2048], P('dp', 'section', 'ctx'), may hold values from -6 to 6
- key_input: bfloat16 [8, 32, 512, 512], P('dp', 'section', 'ctx'), may hold values from -6 to 6
- value_input: bfloat16 [8, 32, 512, 512], P('dp', 'section', 'ctx'), may hold values from -6 to 6
- output_saved: bfloat16 [8, 32, 512, 2048], P('dp', 'section', 'ctx'), may hold values from -6 to 6
- output_gradient: bfloat16 [8, 32, 512, 2048], P('dp', 'section', 'ctx'), may hold values from -6 to 6
- lse: float32 [8, 32, 16, 512], P('dp', 'section', None, 'ctx'), may hold values from 2 to 5
- bias_q: bfloat16 [32, 2048], P('section'), may hold values from -3 to 3
- key_bias: bfloat16 [32, 512], P('section'), may hold values from -3 to 3
- value_bias: bfloat16 [32, 512], P('section'), may hold values from -3 to 3
Outputs:
- recv_q: bfloat16 [8, 32, 512, 2048], P('dp', 'section', 'ctx')
- recv_k: bfloat16 [8, 32, 512, 512], P('dp', 'section', 'ctx')
- recv_v: bfloat16 [8, 32, 512, 512], P('dp', 'section', 'ctx')
- grad_bq: float32 [32, 2048], P('section')
- grad_bk: float32 [32, 512], P('section')
- grad_bv: float32 [32, 512], P('section')
All inputs are finite; a program needn't handle non-finite values.
Results may differ from a plain program's by a relative error of at most 0.0035.
The roundings to bfloat16 on the way count: a program that leaves them out, or rounds other values in their place, can miss the bound.
Values may be sent and summed in bfloat16 or wider, within the bound.
No kernel may reach another device: no remote copies, remote signals or barrier semaphores. Data moves between devices by JAX's collectives and lax.ppermute only.
A program may use at most 32 MiB of HBM per device.

v0:
```python
import functools
import math

import jax
import jax.numpy as jnp
from jax import lax
from jax.experimental import pallas as pl
from jax.experimental.pallas import tpu as pltpu
from jax.sharding import PartitionSpec as P


HEAD_SIZE = 128
ROWS = 128
HALF = ROWS // 2
Q_HEADS = 16
KV_HEADS = 4
Q_OWN = Q_HEADS // 2
KV_OWN = KV_HEADS // 2
GROUP = Q_HEADS // KV_HEADS
SCALE = 1.0 / math.sqrt(HEAD_SIZE)
LOG2E = math.log2(math.e)
AT_Q = 0
AT_G = AT_Q + Q_OWN
AT_K = AT_G + Q_OWN
AT_V = AT_K + KV_OWN
AT_ROW = AT_V + KV_OWN
PACK = AT_ROW + 1
SUM_ROWS = 16
BF16 = jnp.bfloat16
F32 = jnp.float32
LOW = -1e30
KERNEL_VMEM = 24 << 20

SMEM = pl.BlockSpec(memory_space=pltpu.SMEM)
VMEM = pl.BlockSpec(memory_space=pltpu.VMEM)


def call(kernel, outs, n_in, flops=0, moved=0, keep=True, vmem=KERNEL_VMEM):
    keep = len(outs) if keep is True else int(keep)
    outs = [pltpu.VMEM(o.shape, o.dtype) for o in outs[:keep]] + outs[keep:]
    run = pl.pallas_call(
        kernel,
        out_shape=outs,
        in_specs=[SMEM] + [VMEM] * n_in,
        out_specs=[VMEM] * len(outs),
        compiler_params=pltpu.CompilerParams(vmem_limit_bytes=vmem),
        cost_estimate=pl.CostEstimate(flops=flops, bytes_accessed=moved, transcendentals=0),
    )
    return run


def held(x):
    return pltpu.with_memory_space_constraint(x, pltpu.VMEM)


def shape(*dims, dtype=BF16):
    return jax.ShapeDtypeStruct(dims, dtype)


def split3(x):
    a = x.astype(BF16)
    rest = x - a.astype(F32)
    b = rest.astype(BF16)
    return a, b, (rest - b.astype(F32)).astype(BF16)


def prep_kernel(at, q, k, v, o, g, lse, bq, bk, bv, own, send, kv1, kv2):
    core = at[0] % 2
    for pack, side in ((own, core), (send, 1 - core)):
        base = pl.multiple_of(side * (Q_OWN * HEAD_SIZE), Q_OWN * HEAD_SIZE)
        kv_base = pl.multiple_of(side * (KV_OWN * HEAD_SIZE), KV_OWN * HEAD_SIZE)
        deltas = []
        for h in range(Q_OWN):
            cols = pl.ds(base + h * HEAD_SIZE, HEAD_SIZE)
            pack[AT_Q + h] = (q[:, cols].astype(F32) + bq[:, cols].astype(F32)).astype(BF16)
            grad = g[:, cols]
            pack[AT_G + h] = grad
            deltas.append(
                jnp.sum(grad.astype(F32) * o[:, cols].astype(F32), axis=1, keepdims=True)
            )
        for h in range(KV_OWN):
            cols = pl.ds(kv_base + h * HEAD_SIZE, HEAD_SIZE)
            kb = (k[:, cols].astype(F32) + bk[:, cols].astype(F32)).astype(BF16)
            vb = (v[:, cols].astype(F32) + bv[:, cols].astype(F32)).astype(BF16)
            pack[AT_K + h] = kb
            pack[AT_V + h] = vb
            to = 0 if pack is own else 1
            kv1[to, h] = kb[:HALF]
            kv2[to, h] = kb[HALF:]
            kv1[to, KV_OWN + h] = vb[:HALF]
            kv2[to, KV_OWN + h] = vb[HALF:]
        delta = jnp.concatenate(deltas + [jnp.zeros((ROWS, HEAD_SIZE - Q_OWN), F32)], axis=1).T
        heads = pl.ds(pl.multiple_of(side * Q_OWN, Q_OWN), Q_OWN)
        stats = jnp.concatenate(
            [p.astype(F32) for p in split3(lse[heads, :])]
            + [p.astype(F32) for p in split3(delta[:Q_OWN])]
            + [jnp.zeros((ROWS - 6 * Q_OWN, HEAD_SIZE), F32)],
            axis=0,
        )
        pack[AT_ROW] = stats.astype(BF16)


def row_stats(own, recv):
    def one(pack):
        s = pack[AT_ROW].astype(F32)
        n = Q_OWN
        lse = (s[:n] + s[n : 2 * n]) + s[2 * n : 3 * n]
        delta = (s[3 * n : 4 * n] + s[4 * n : 5 * n]) + s[5 * n : 6 * n]
        return lse * LOG2E, delta

    (la, da), (lb, db) = one(own), one(recv)
    return jnp.concatenate([la, lb], axis=1), jnp.concatenate([da, db], axis=1)


def positions(index, dim, ctx_count, alternate):
    i = lax.broadcasted_iota(jnp.int32, (2 * ROWS, 2 * ROWS), dim)
    part = i // HALF
    late = part // 2 if alternate else part % 2
    other = part % 2 if alternate else part // 2
    block = jnp.where(other == 1, index + 1 - 2 * (index % 2), index)
    half = jnp.where(late == 1, 2 * ctx_count - 1 - block, block)
    return half * HALF + i % HALF


def head_terms(q, g, k, v, bias, lse, delta):
    s = lax.dot_general(k, q, (((1,), (1,)), ((), ())), preferred_element_type=F32)
    dp = lax.dot_general(v, g, (((1,), (1,)), ((), ())), preferred_element_type=F32)
    p = jnp.exp2(s * (SCALE * LOG2E) + (bias - lse))
    ds = (p * (dp - delta)).astype(BF16)
    p = p.astype(BF16)
    gv = jnp.dot(p, g, preferred_element_type=F32)
    gk = jnp.dot(ds, q, preferred_element_type=F32)
    gq = lax.dot_general(ds, k, (((0,), (0,)), ((), ())), preferred_element_type=F32)
    return gq, gk, gv


def local_kernel(at, own, recv, gq_out, gkv_out, *, ctx_count):
    kpos = positions(at[0], 0, ctx_count, False)
    qpos = positions(at[0], 1, ctx_count, False)
    bias = jnp.where(kpos <= qpos, 0.0, LOW)
    lse, delta = row_stats(own, recv)
    for kv in range(KV_OWN):
        k = jnp.concatenate([own[AT_K + kv], recv[AT_K + kv]], axis=0)
        v = jnp.concatenate([own[AT_V + kv], recv[AT_V + kv]], axis=0)
        gk = gv = None
        for j in range(GROUP):
            h = kv * GROUP + j
            q = jnp.concatenate([own[AT_Q + h], recv[AT_Q + h]], axis=0)
            g = jnp.concatenate([own[AT_G + h], recv[AT_G + h]], axis=0)
            tq, tk, tv = head_terms(q, g, k, v, bias, lse[h : h + 1], delta[h : h + 1])
            gq_out[h] = tq
            gk = tk if gk is None else gk + tk
            gv = tv if gv is None else gv + tv
        gkv_out[kv] = gk * SCALE
        gkv_out[KV_OWN + kv] = gv


def remote_kernel(
    at, own, recv, kv1, kv2, cross, gq_in, gkv_in, gq_same, gq_other, gr1, gr2, sums, *, ctx_count
):
    far_kv = (kv1.at[0], cross.at[0], kv2.at[0], cross.at[1])
    totals = []
    far = (at[0] + ctx_count // 2) % ctx_count
    kpos = positions(far, 0, ctx_count, True)
    qpos = positions(at[0], 1, ctx_count, False)
    bias = jnp.where(kpos <= qpos, 0.0, LOW)
    lse, delta = row_stats(own, recv)
    for kv in range(KV_OWN):
        k = jnp.concatenate([r[kv] for r in far_kv], axis=0)
        v = jnp.concatenate([r[KV_OWN + kv] for r in far_kv], axis=0)
        gk = gv = None
        for j in range(GROUP):
            h = kv * GROUP + j
            q = jnp.concatenate([own[AT_Q + h], recv[AT_Q + h]], axis=0)
            g = jnp.concatenate([own[AT_G + h], recv[AT_G + h]], axis=0)
            tq, tk, tv = head_terms(q, g, k, v, bias, lse[h : h + 1], delta[h : h + 1])
            gq = (gq_in[h] + tq) * SCALE
            gq_same[h] = gq[:ROWS].astype(BF16)
            gq_other[h] = gq[ROWS:].astype(BF16)
            totals.append((h, jnp.sum(gq, axis=0, keepdims=True)))
            gk = tk if gk is None else gk + tk
            gv = tv if gv is None else gv + tv
        for at_row, t in ((kv, gk * SCALE), (KV_OWN + kv, gv)):
            gr1[at_row] = t[:ROWS]
            gr2[at_row] = t[ROWS:]
            total = jnp.sum(t, axis=0, keepdims=True) + jnp.sum(
                gkv_in[at_row], axis=0, keepdims=True
            )
            totals.append((Q_OWN + at_row, total))
    pad = SUM_ROWS - len(totals)
    totals = [t for _, t in sorted(totals, key=lambda t: t[0])] + [jnp.zeros((pad, HEAD_SIZE), F32)]
    sums[...] = jnp.broadcast_to(jnp.concatenate(totals, axis=0)[None], sums.shape)


def cross_kernel(at, kv1, kv2, out):
    out[0] = kv1[1]
    out[1] = kv2[1]


def kv_kernel(at, gkv, r1, r2, same, other):
    for i in range(2 * KV_OWN):
        same[i, :HALF] = (gkv[i, :HALF] + r1[i, :HALF]).astype(BF16)
        same[i, HALF:] = (gkv[i, HALF:ROWS] + r2[i, :HALF]).astype(BF16)
        other[i, :HALF] = (gkv[i, ROWS : ROWS + HALF] + r1[i, HALF:]).astype(BF16)
        other[i, HALF:] = (gkv[i, ROWS + HALF :] + r2[i, HALF:]).astype(BF16)


def join_q_kernel(at, same, other, out):
    core = at[0] % 2
    for part, side in ((same, core), (other, 1 - core)):
        base = pl.multiple_of(side * (Q_OWN * HEAD_SIZE), Q_OWN * HEAD_SIZE)
        for h in range(Q_OWN):
            out[:, pl.ds(base + h * HEAD_SIZE, HEAD_SIZE)] = part[h]


def join_kv_kernel(at, same, other, out_k, out_v):
    core = at[0] % 2
    for part, side in ((same, core), (other, 1 - core)):
        base = pl.multiple_of(side * (KV_OWN * HEAD_SIZE), KV_OWN * HEAD_SIZE)
        for h in range(KV_OWN):
            cols = pl.ds(base + h * HEAD_SIZE, HEAD_SIZE)
            out_k[:, cols] = part[h]
            out_v[:, cols] = part[KV_OWN + h]


def join_sums_kernel(at, parts, out_q, out_k, out_v):
    ctx_count, dp_count = parts.shape[:2]
    for core in range(2):
        total = None
        for c in range(core, ctx_count, 2):
            for r in range(dp_count):
                total = parts[c, r] if total is None else total + parts[c, r]
        for h in range(Q_OWN):
            at_col = (core * Q_OWN + h) * HEAD_SIZE
            out_q[:, at_col : at_col + HEAD_SIZE] = total[h : h + 1]
        for h in range(KV_OWN):
            at_col = (core * KV_OWN + h) * HEAD_SIZE
            row = Q_OWN + h
            out_k[:, at_col : at_col + HEAD_SIZE] = total[row : row + 1]
            row += KV_OWN
            out_v[:, at_col : at_col + HEAD_SIZE] = total[row : row + 1]


def swapped(value, axis, bit):
    size = lax.axis_size(axis)
    return lax.ppermute(value, axis, [(i, i ^ bit) for i in range(size)])


def body(q_in, k_in, v_in, o_in, g_in, lse, bq, bk, bv):
    n = lax.axis_size("ctx")
    at = lax.axis_index("ctx").astype(jnp.int32).reshape(1)
    chips = n // 2
    blocks = lambda count, rows=ROWS, dtype=BF16: shape(count, rows, HEAD_SIZE, dtype=dtype)

    dp = lax.axis_size("dp")
    own, send, kv1, kv2 = call(
        prep_kernel,
        [blocks(PACK), blocks(PACK)] + [shape(2, 2 * KV_OWN, HALF, HEAD_SIZE)] * 2,
        9,
        moved=4 << 20,
        keep=2,
        vmem=60 << 20,
    )(at, q_in[0, 0], k_in[0, 0], v_in[0, 0], o_in[0, 0], g_in[0, 0], lse[0, 0], bq, bk, bv)

    up = [(i + chips, i) for i in range(chips)]
    down = [(i, i + chips) for i in range(chips)]
    kv1 = held(swapped(kv1, "ctx", chips))
    kv2 = held(lax.ppermute(kv2, "ctx", up))
    recv = held(swapped(send, "ctx", 1))
    own = held(own)

    gq, gkv = call(
        functools.partial(local_kernel, ctx_count=n),
        [blocks(Q_OWN, 2 * ROWS, F32), blocks(2 * KV_OWN, 2 * ROWS, F32)],
        2,
        flops=700_000_000,
        moved=3 << 20,
    )(at, own, recv)
    gq, gkv = held(gq), held(gkv)
    (cross,) = call(cross_kernel, [shape(2, 2 * KV_OWN, HALF, HEAD_SIZE)], 2)(at, kv1, kv2)
    cross = held(swapped(cross, "ctx", 1))
    gq_same, gq_other, gr1, gr2, sums = call(
        functools.partial(remote_kernel, ctx_count=n),
        [blocks(Q_OWN)] * 2
        + [blocks(2 * KV_OWN, ROWS, F32)] * 2
        + [shape(n * dp, SUM_ROWS, HEAD_SIZE, dtype=F32)],
        7,
        flops=700_000_000,
        moved=4 << 20,
        keep=4,
    )(at, own, recv, kv1, kv2, cross, gq, gkv)

    r1 = held(swapped(gr1, "ctx", chips))
    r2 = held(lax.ppermute(gr2, "ctx", down))

    def before(x, bit):
        pairs = []
        for s in range(1, lax.axis_size("section")):
            pairs += [(s * n + c, (s - 1) * n + (c ^ bit)) for c in range(n)]
        return held(lax.ppermute(x, ("section", "ctx"), pairs))

    gq_same, gq_other = before(gq_same, 0), before(gq_other, 1)
    sums = lax.all_to_all(sums, ("ctx", "dp"), 0, 0, tiled=True)
    sum_q, sum_k, sum_v = call(
        join_sums_kernel,
        [
            shape(1, Q_HEADS * HEAD_SIZE, dtype=F32),
            shape(1, KV_HEADS * HEAD_SIZE, dtype=F32),
            shape(1, KV_HEADS * HEAD_SIZE, dtype=F32),
        ],
        1,
        keep=False,
    )(at, held(sums.reshape(n, dp, SUM_ROWS, HEAD_SIZE)))
    kv_same, kv_other = call(kv_kernel, [blocks(2 * KV_OWN)] * 2, 3, moved=2 << 20)(at, gkv, r1, r2)
    kv_same, kv_other = before(kv_same, 0), before(kv_other, 1)
    (recv_q,) = call(
        join_q_kernel, [shape(ROWS, Q_HEADS * HEAD_SIZE)], 2, moved=1 << 20, keep=False
    )(at, gq_same, gq_other)
    recv_k, recv_v = call(
        join_kv_kernel, [shape(ROWS, KV_HEADS * HEAD_SIZE)] * 2, 2, moved=1 << 19, keep=False
    )(at, kv_same, kv_other)
    return (recv_q[None, None], recv_k[None, None], recv_v[None, None], sum_q, sum_k, sum_v)


def solution(mesh):
    return jax.shard_map(
        body,
        mesh=mesh,
        in_specs=(
            P("dp", "section", "ctx", None),
            P("dp", "section", "ctx", None),
            P("dp", "section", "ctx", None),
            P("dp", "section", "ctx", None),
            P("dp", "section", "ctx", None),
            P("dp", "section", None, "ctx"),
            P("section", None),
            P("section", None),
            P("section", None),
        ),
        out_specs=(
            P("dp", "section", "ctx", None),
            P("dp", "section", "ctx", None),
            P("dp", "section", "ctx", None),
            P("section", None),
            P("section", None),
            P("section", None),
        ),
        check_vma=False,
    )
```

profile of v0, /device:TPU:83, one launch (start us, length us, event | category | flops | bytes accessed | tf_op | source)
XLA Modules:
  0.0 108.6 jit_solution(12055831274151838131)
XLA Ops:
  0.6 2.7 %shard_map.136 = (bf16[21,128,128]{2,1,0:T(8,128)(2,1)S(1)}, bf16[21,128,128]{2,1,0:T(8,128)(2,1)S(1)}, bf16[2,4,64,128]{3,2,1,0:T(8,128)(2,1)}, bf16[2,4,64,128]{3,2,1,0:T(8,128)(2,1)}) custom-call(s32[1]{0:T(128)} %bitcast.at, bf16[128,2048]{1,0:T(8,128)(2,1)} %bitcast.13, bf16[128,512]{1,0:T(8,128)(2,1)} %bitcast.16, bf16[128,512]{1,0:T(8,128)(2,1)} %bitcast.17, ...), custom_call_target="tpu_custom_call" | custom-call | bytes 4194304 | tf_op jit(solution)/shard_map/pallas_call | solution.py:256
  3.3 2.6 %collective-permute-start = (bf16[21,128,128]{2,1,0:T(8,128)(2,1)S(1)}, bf16[21,128,128]{2,1,0:T(8,128)(2,1)S(1)}, u32[]{:S(2)}, u32[]{:S(2)}) collective-permute-start(bf16[21,128,128]{2,1,0:T(8,128)(2,1)S(1)} %get-tuple-element.25), channel_id=1, source_target_pairs={{0,8},{8,0},{16,24},{24,16},{1,9},{9,1},{17,25},{25,17},{2,10},{10... | collective-permute-start | bytes 2064392 | tf_op jit(solution)/shard_map/ppermute | solution.py:246
  5.9 14.3 %collective-permute-start.1 = (bf16[2,4,64,128]{3,2,1,0:T(8,128)(2,1)}, bf16[2,4,64,128]{3,2,1,0:T(8,128)(2,1)S(1)}, u32[]{:S(2)}, u32[]{:S(2)}) collective-permute-start(bf16[2,4,64,128]{3,2,1,0:T(8,128)(2,1)} %get-tuple-element.26), channel_id=1, source_target_pairs={{0,16},{8,24},{16,0},{24,8},{1,17},{9,25},{17,1},{25,9},{2,18},{10... | collective-permute-start | bytes 393224 | tf_op jit(solution)/shard_map/ppermute | solution.py:246
  20.2 1.3 %collective-permute-start.2 = (bf16[2,4,64,128]{3,2,1,0:T(8,128)(2,1)}, bf16[2,4,64,128]{3,2,1,0:T(8,128)(2,1)S(1)}, u32[]{:S(2)}, u32[]{:S(2)}) collective-permute-start(bf16[2,4,64,128]{3,2,1,0:T(8,128)(2,1)} %get-tuple-element.27), channel_id=1, source_target_pairs={{16,0},{24,8},{17,1},{25,9},{18,2},{26,10},{19,3},{27,11},{20,4},{... | collective-permute-start | bytes 393224 | tf_op jit(solution)/shard_map/ppermute | solution.py:268
  21.5 2.8 %collective-permute-done.1.kv1 = bf16[2,4,64,128]{3,2,1,0:T(8,128)(2,1)S(1)} collective-permute-done((bf16[2,4,64,128]{3,2,1,0:T(8,128)(2,1)}, bf16[2,4,64,128]{3,2,1,0:T(8,128)(2,1)S(1)}, u32[]{:S(2)}, u32[]{:S(2)}) %collective-permute-start.1) | collective-permute-done | bytes 131104 | tf_op jit(solution)/shard_map/ppermute | solution.py:246
  24.2 9.5 %collective-permute-done.2.kv2 = bf16[2,4,64,128]{3,2,1,0:T(8,128)(2,1)S(1)} collective-permute-done((bf16[2,4,64,128]{3,2,1,0:T(8,128)(2,1)}, bf16[2,4,64,128]{3,2,1,0:T(8,128)(2,1)S(1)}, u32[]{:S(2)}, u32[]{:S(2)}) %collective-permute-start.2) | collective-permute-done | bytes 131104 | tf_op jit(solution)/shard_map/ppermute | solution.py:268
  33.8 3.1 %collective-permute-start.3 = (bf16[2,4,64,128]{3,2,1,0:T(8,128)(2,1)S(1)}, bf16[2,4,64,128]{3,2,1,0:T(8,128)(2,1)S(1)}, u32[]{:S(2)}, u32[]{:S(2)}) collective-permute-start(bf16[2,4,64,128]{3,2,1,0:T(8,128)(2,1)S(1)} %shard_map.137), channel_id=1, source_target_pairs={{0,8},{8,0},{16,24},{24,16},{1,9},{9,1},{17,25},{25,17},{2,10},{10... | collective-permute-start | bytes 393224 | tf_op jit(solution)/shard_map/ppermute | solution.py:246
  36.9 0.0 collective-permute-done.recv
  36.9 2.7 %shard_map.138 = (f32[8,256,128]{2,1,0:T(8,128)S(1)}, f32[4,256,128]{2,1,0:T(8,128)S(1)}) custom-call(s32[1]{0:T(128)} %bitcast.at, bf16[21,128,128]{2,1,0:T(8,128)(2,1)S(1)} %get-tuple-element.24.own, bf16[21,128,128]{2,1,0:T(8,128)(2,1)S(1)} %collective-permute-done.recv), custom_call_target="tpu_custom_call" | custom-call | flops 700000000 | bytes 3145728 | tf_op jit(solution)/shard_map/pallas_call | solution.py:272
  39.6 0.0 collective-permute-done.3.cross
  39.6 3.4 %shard_map.139 = (bf16[8,128,128]{2,1,0:T(8,128)(2,1)S(1)}, bf16[8,128,128]{2,1,0:T(8,128)(2,1)S(1)}, f32[4,128,128]{2,1,0:T(8,128)S(1)}, f32[4,128,128]{2,1,0:T(8,128)S(1)}, f32[32,16,128]{2,1,0:T(8,128)}) custom-call(s32[1]{0:T(128)} %bitcast.at, bf16[21,128,128]{2,1,0:T(8,128)(2,1)S(1)} %get-tuple-element.24.own, ...), custom_call_target="tpu_custom_call" | custom-call | flops 700000000 | bytes 4194304 | tf_op jit(solution)/shard_map/pallas_call | solution.py:282
  43.0 7.2 %all-to-all-start = ((f32[32,16,128]{2,1,0:T(8,128)}), f32[32,16,128]{2,1,0:T(8,128)S(1)}, u32[]{:S(2)}, u32[]{:S(2)}) async-start(f32[32,16,128]{2,1,0:T(8,128)} %get-tuple-element.38), calls=%async_computation | async-start | bytes 524288 | tf_op jit(solution)/shard_map/all_to_all | solution.py:303
  50.2 7.0 %collective-permute-start.6 = (f32[4,128,128]{2,1,0:T(8,128)S(1)}, f32[4,128,128]{2,1,0:T(8,128)S(1)}, u32[]{:S(2)}, u32[]{:S(2)}) collective-permute-start(f32[4,128,128]{2,1,0:T(8,128)S(1)} %get-tuple-element.32), channel_id=1, source_target_pairs={{0,16},{8,24},{16,0},{24,8},{1,17},{9,25},{17,1},{25,9},{2,18},{10... | collective-permute-start | bytes 786440 | tf_op jit(solution)/shard_map/ppermute | solution.py:246
  57.2 2.2 %collective-permute-start.7 = (f32[4,128,128]{2,1,0:T(8,128)S(1)}, f32[4,128,128]{2,1,0:T(8,128)S(1)}, u32[]{:S(2)}, u32[]{:S(2)}) collective-permute-start(f32[4,128,128]{2,1,0:T(8,128)S(1)} %get-tuple-element.33), channel_id=1, source_target_pairs={{0,16},{8,24},{1,17},{9,25},{2,18},{10,26},{3,19},{11,27},{4,20},{... | collective-permute-start | bytes 786440 | tf_op jit(solution)/shard_map/ppermute | solution.py:294
  59.4 5.6 %collective-permute-start.4 = (bf16[8,128,128]{2,1,0:T(8,128)(2,1)S(1)}, bf16[8,128,128]{2,1,0:T(8,128)(2,1)S(1)}, u32[]{:S(2)}, u32[]{:S(2)}) collective-permute-start(bf16[8,128,128]{2,1,0:T(8,128)(2,1)S(1)} %get-tuple-element.30), channel_id=1, source_target_pairs={{32,0},{40,8},{48,16},{56,24},{64,32},{72,40},{80,48},{88,56},{96,... | collective-permute-start | bytes 786440 | tf_op jit(solution)/shard_map/ppermute | solution.py:300
  65.0 4.4 %collective-permute-start.5 = (bf16[8,128,128]{2,1,0:T(8,128)(2,1)S(1)}, bf16[8,128,128]{2,1,0:T(8,128)(2,1)S(1)}, u32[]{:S(2)}, u32[]{:S(2)}) collective-permute-start(bf16[8,128,128]{2,1,0:T(8,128)(2,1)S(1)} %get-tuple-element.31), channel_id=1, source_target_pairs={{32,8},{40,0},{48,24},{56,16},{64,40},{72,32},{80,56},{88,48},{96,... | collective-permute-start | bytes 786440 | tf_op jit(solution)/shard_map/ppermute | solution.py:300
  69.4 15.0 %collective-permute-done.6.r1 = f32[4,128,128]{2,1,0:T(8,128)S(1)} collective-permute-done((f32[4,128,128]{2,1,0:T(8,128)S(1)}, f32[4,128,128]{2,1,0:T(8,128)S(1)}, u32[]{:S(2)}, u32[]{:S(2)}) %collective-permute-start.6) | collective-permute-done | bytes 262176 | tf_op jit(solution)/shard_map/ppermute | solution.py:246
  84.4 3.8 %collective-permute-done.7.r2 = f32[4,128,128]{2,1,0:T(8,128)S(1)} collective-permute-done((f32[4,128,128]{2,1,0:T(8,128)S(1)}, f32[4,128,128]{2,1,0:T(8,128)S(1)}, u32[]{:S(2)}, u32[]{:S(2)}) %collective-permute-start.7) | collective-permute-done | bytes 262176 | tf_op jit(solution)/shard_map/ppermute | solution.py:294
  88.3 0.1 shard_map.141
  88.3 1.9 %collective-permute-start.8 = (bf16[4,128,128]{2,1,0:T(8,128)(2,1)S(1)}, bf16[4,128,128]{2,1,0:T(8,128)(2,1)S(1)}, u32[]{:S(2)}, u32[]{:S(2)}) collective-permute-start(bf16[4,128,128]{2,1,0:T(8,128)(2,1)S(1)} %get-tuple-element.34), channel_id=1, source_target_pairs={{32,0},{40,8},{48,16},{56,24},{64,32},{72,40},{80,48},{88,56},{96,... | collective-permute-start | bytes 393224 | tf_op jit(solution)/shard_map/ppermute | solution.py:300
  90.3 13.7 %collective-permute-start.9 = (bf16[4,128,128]{2,1,0:T(8,128)(2,1)S(1)}, bf16[4,128,128]{2,1,0:T(8,128)(2,1)S(1)}, u32[]{:S(2)}, u32[]{:S(2)}) collective-permute-start(bf16[4,128,128]{2,1,0:T(8,128)(2,1)S(1)} %get-tuple-element.35), channel_id=1, source_target_pairs={{32,8},{40,0},{48,24},{56,16},{64,40},{72,32},{80,56},{88,48},{96,... | collective-permute-start | bytes 393224 | tf_op jit(solution)/shard_map/ppermute | solution.py:300
  103.9 0.0 collective-permute-done.4.same
  103.9 0.0 collective-permute-done.5.other
  104.0 0.9 shard_map.140
  104.9 0.0 collective-permute-done.8.same
  104.9 2.3 %collective-permute-done.9.other = bf16[4,128,128]{2,1,0:T(8,128)(2,1)S(1)} collective-permute-done((bf16[4,128,128]{2,1,0:T(8,128)(2,1)S(1)}, bf16[4,128,128]{2,1,0:T(8,128)(2,1)S(1)}, u32[]{:S(2)}, u32[]{:S(2)}) %collective-permute-start.9) | collective-permute-done | bytes 131104 | tf_op jit(solution)/shard_map/ppermute | solution.py:300
  107.2 0.7 shard_map.142
  107.9 0.0 all-to-all-done
  108.0 0.6 shard_map.143
  (1 shorter events, 0.0 us)
Async XLA Ops:
  3.3 33.5 %collective-permute-start = (bf16[21,128,128]{2,1,0:T(8,128)(2,1)S(1)}, bf16[21,128,128]{2,1,0:T(8,128)(2,1)S(1)}, u32[]{:S(2)}, u32[]{:S(2)}) collective-permute-start(bf16[21,128,128]{2,1,0:T(8,128)(2,1)S(1)} %get-tuple-element.25), channel_id=1, source_target_pairs={{0,8},{8,0},{16,24},{24,16},{1,9},{9,1},{17,25},{25,17},{2,10},{10... | collective-permute-start | bytes 2064392 | tf_op jit(solution)/shard_map/ppermute | solution.py:246
  5.9 18.3 %collective-permute-start.1 = (bf16[2,4,64,128]{3,2,1,0:T(8,128)(2,1)}, bf16[2,4,64,128]{3,2,1,0:T(8,128)(2,1)S(1)}, u32[]{:S(2)}, u32[]{:S(2)}) collective-permute-start(bf16[2,4,64,128]{3,2,1,0:T(8,128)(2,1)} %get-tuple-element.26), channel_id=1, source_target_pairs={{0,16},{8,24},{16,0},{24,8},{1,17},{9,25},{17,1},{25,9},{2,18},{10... | collective-permute-start | bytes 393224 | tf_op jit(solution)/shard_map/ppermute | solution.py:246
  20.2 13.6 %collective-permute-start.2 = (bf16[2,4,64,128]{3,2,1,0:T(8,128)(2,1)}, bf16[2,4,64,128]{3,2,1,0:T(8,128)(2,1)S(1)}, u32[]{:S(2)}, u32[]{:S(2)}) collective-permute-start(bf16[2,4,64,128]{3,2,1,0:T(8,128)(2,1)} %get-tuple-element.27), channel_id=1, source_target_pairs={{16,0},{24,8},{17,1},{25,9},{18,2},{26,10},{19,3},{27,11},{20,4},{... | collective-permute-start | bytes 393224 | tf_op jit(solution)/shard_map/ppermute | solution.py:268
  33.8 5.8 %collective-permute-start.3 = (bf16[2,4,64,128]{3,2,1,0:T(8,128)(2,1)S(1)}, bf16[2,4,64,128]{3,2,1,0:T(8,128)(2,1)S(1)}, u32[]{:S(2)}, u32[]{:S(2)}) collective-permute-start(bf16[2,4,64,128]{3,2,1,0:T(8,128)(2,1)S(1)} %shard_map.137), channel_id=1, source_target_pairs={{0,8},{8,0},{16,24},{24,16},{1,9},{9,1},{17,25},{25,17},{2,10},{10... | collective-permute-start | bytes 393224 | tf_op jit(solution)/shard_map/ppermute | solution.py:246
  43.0 65.0 %all-to-all-start = ((f32[32,16,128]{2,1,0:T(8,128)}), f32[32,16,128]{2,1,0:T(8,128)S(1)}, u32[]{:S(2)}, u32[]{:S(2)}) async-start(f32[32,16,128]{2,1,0:T(8,128)} %get-tuple-element.38), calls=%async_computation | async-start | bytes 524288 | tf_op jit(solution)/shard_map/all_to_all | solution.py:303
  50.2 34.3 %collective-permute-start.6 = (f32[4,128,128]{2,1,0:T(8,128)S(1)}, f32[4,128,128]{2,1,0:T(8,128)S(1)}, u32[]{:S(2)}, u32[]{:S(2)}) collective-permute-start(f32[4,128,128]{2,1,0:T(8,128)S(1)} %get-tuple-element.32), channel_id=1, source_target_pairs={{0,16},{8,24},{16,0},{24,8},{1,17},{9,25},{17,1},{25,9},{2,18},{10... | collective-permute-start | bytes 786440 | tf_op jit(solution)/shard_map/ppermute | solution.py:246
  57.2 31.0 %collective-permute-start.7 = (f32[4,128,128]{2,1,0:T(8,128)S(1)}, f32[4,128,128]{2,1,0:T(8,128)S(1)}, u32[]{:S(2)}, u32[]{:S(2)}) collective-permute-start(f32[4,128,128]{2,1,0:T(8,128)S(1)} %get-tuple-element.33), channel_id=1, source_target_pairs={{0,16},{8,24},{1,17},{9,25},{2,18},{10,26},{3,19},{11,27},{4,20},{... | collective-permute-start | bytes 786440 | tf_op jit(solution)/shard_map/ppermute | solution.py:294
  59.4 44.6 %collective-permute-start.4 = (bf16[8,128,128]{2,1,0:T(8,128)(2,1)S(1)}, bf16[8,128,128]{2,1,0:T(8,128)(2,1)S(1)}, u32[]{:S(2)}, u32[]{:S(2)}) collective-permute-start(bf16[8,128,128]{2,1,0:T(8,128)(2,1)S(1)} %get-tuple-element.30), channel_id=1, source_target_pairs={{32,0},{40,8},{48,16},{56,24},{64,32},{72,40},{80,48},{88,56},{96,... | collective-permute-start | bytes 786440 | tf_op jit(solution)/shard_map/ppermute | solution.py:300
  65.0 38.9 %collective-permute-start.5 = (bf16[8,128,128]{2,1,0:T(8,128)(2,1)S(1)}, bf16[8,128,128]{2,1,0:T(8,128)(2,1)S(1)}, u32[]{:S(2)}, u32[]{:S(2)}) collective-permute-start(bf16[8,128,128]{2,1,0:T(8,128)(2,1)S(1)} %get-tuple-element.31), channel_id=1, source_target_pairs={{32,8},{40,0},{48,24},{56,16},{64,40},{72,32},{80,56},{88,48},{96,... | collective-permute-start | bytes 786440 | tf_op jit(solution)/shard_map/ppermute | solution.py:300
  88.3 16.6 %collective-permute-start.8 = (bf16[4,128,128]{2,1,0:T(8,128)(2,1)S(1)}, bf16[4,128,128]{2,1,0:T(8,128)(2,1)S(1)}, u32[]{:S(2)}, u32[]{:S(2)}) collective-permute-start(bf16[4,128,128]{2,1,0:T(8,128)(2,1)S(1)} %get-tuple-element.34), channel_id=1, source_target_pairs={{32,0},{40,8},{48,16},{56,24},{64,32},{72,40},{80,48},{88,56},{96,... | collective-permute-start | bytes 393224 | tf_op jit(solution)/shard_map/ppermute | solution.py:300
  90.3 16.9 %collective-permute-start.9 = (bf16[4,128,128]{2,1,0:T(8,128)(2,1)S(1)}, bf16[4,128,128]{2,1,0:T(8,128)(2,1)S(1)}, u32[]{:S(2)}, u32[]{:S(2)}) collective-permute-start(bf16[4,128,128]{2,1,0:T(8,128)(2,1)S(1)} %get-tuple-element.35), channel_id=1, source_target_pairs={{32,8},{40,0},{48,24},{56,16},{64,40},{72,32},{80,56},{88,48},{96,... | collective-permute-start | bytes 393224 | tf_op jit(solution)/shard_map/ppermute | solution.py:300
where the time goes:
time: 109 us
  starting transfers between devices  63.2 us (58%)
  waiting for transfers between devices  33.4 us (31%)
  Pallas kernels  11.2 us (10%)
    ppermute x4, starting transfers between devices, swapped(): return lax.ppermute(value, axis, [(i, i ^ bit) for i in range(size)])  27 us
    ppermute x4, starting transfers between devices, before(): return held(lax.ppermute(x, ('section', 'ctx'), pairs))  25.6 us
    ppermute x4, waiting for transfers between devices, swapped(): return lax.ppermute(value, axis, [(i, i ^ bit) for i in range(size)])  17.7 us
    ppermute x1, waiting for transfers between devices, body(): kv2 = held(lax.ppermute(kv2, 'ctx', up))  9.51 us
    all_to_all x1, starting transfers between devices, body(): sums = lax.all_to_all(sums, ('ctx', 'dp'), 0, 0, tiled=True)  7.18 us
    ppermute x1, waiting for transfers between devices, body(): r2 = held(lax.ppermute(gr2, 'ctx', down))  3.84 us
    pallas_call x1, Pallas kernels, body(): call(functools.partial(remote_kernel, ctx_count=n), [blocks(Q_OWN)] * 2 +...  3.4 us
    pallas_call x1, Pallas kernels, body(): call(functools.partial(local_kernel, ctx_count=n), [blocks(Q_OWN, 2 * ROW...  2.7 us
  transfers between devices with their start and end apart: 11, of which 5 were waited for; matrix products, arithmetic and copies ran while one was open for 0% of the time, Pallas kernels for 4%

commit v1 on v0

--- a/solution.py
+++ b/solution.py
@@ -64,7 +64,7 @@
     return a, b, (rest - b.astype(F32)).astype(BF16)
 
 
-def prep_kernel(at, q, k, v, o, g, lse, bq, bk, bv, own, send, kv1, kv2):
+def prep_kernel(at, q, k, v, o, g, lse, bq, bk, bv, own, send, kvz):
     core = at[0] % 2
     for pack, side in ((own, core), (send, 1 - core)):
         base = pl.multiple_of(side * (Q_OWN * HEAD_SIZE), Q_OWN * HEAD_SIZE)
@@ -85,10 +85,10 @@
             pack[AT_K + h] = kb
             pack[AT_V + h] = vb
             to = 0 if pack is own else 1
-            kv1[to, h] = kb[:HALF]
-            kv2[to, h] = kb[HALF:]
-            kv1[to, KV_OWN + h] = vb[:HALF]
-            kv2[to, KV_OWN + h] = vb[HALF:]
+            for late in range(2):
+                rows = slice(late * HALF, (late + 1) * HALF)
+                kvz[to, late, h] = kb[rows]
+                kvz[to, late, KV_OWN + h] = vb[rows]
         delta = jnp.concatenate(deltas + [jnp.zeros((ROWS, HEAD_SIZE - Q_OWN), F32)], axis=1).T
         heads = pl.ds(pl.multiple_of(side * Q_OWN, Q_OWN), Q_OWN)
         stats = jnp.concatenate(
@@ -134,7 +134,7 @@
     return gq, gk, gv
 
 
-def local_kernel(at, own, recv, gq_out, gkv_out, *, ctx_count):
+def local_kernel(at, own, recv, gq_out, same, other, kv_sums, *, ctx_count):
     kpos = positions(at[0], 0, ctx_count, False)
     qpos = positions(at[0], 1, ctx_count, False)
     bias = jnp.where(kpos <= qpos, 0.0, LOW)
@@ -151,17 +151,19 @@
             gq_out[h] = tq
             gk = tk if gk is None else gk + tk
             gv = tv if gv is None else gv + tv
-        gkv_out[kv] = gk * SCALE
-        gkv_out[KV_OWN + kv] = gv
+        for row, t in ((kv, gk * SCALE), (KV_OWN + kv, gv)):
+            same[row] = t[:ROWS]
+            other[row] = t[ROWS:]
+            kv_sums[row : row + 1, :] = jnp.sum(t, axis=0, keepdims=True)
 
 
 def remote_kernel(
-    at, own, recv, kv1, kv2, cross, gq_in, gkv_in, gq_same, gq_other, gr1, gr2, sums, *, ctx_count
+    at, own, recv, far, cross, gq_in, kv_sums, gq_same, gq_other, r1s, r1x, r2s, r2x, sums, *, ctx_count
 ):
-    far_kv = (kv1.at[0], cross.at[0], kv2.at[0], cross.at[1])
+    far_kv = (far.at[0, 0], cross.at[0], far.at[0, 1], cross.at[1])
     totals = []
-    far = (at[0] + ctx_count // 2) % ctx_count
-    kpos = positions(far, 0, ctx_count, True)
+    far_index = (at[0] + ctx_count // 2) % ctx_count
+    kpos = positions(far_index, 0, ctx_count, True)
     qpos = positions(at[0], 1, ctx_count, False)
     bias = jnp.where(kpos <= qpos, 0.0, LOW)
     lse, delta = row_stats(own, recv)
@@ -180,29 +182,18 @@
             totals.append((h, jnp.sum(gq, axis=0, keepdims=True)))
             gk = tk if gk is None else gk + tk
             gv = tv if gv is None else gv + tv
-        for at_row, t in ((kv, gk * SCALE), (KV_OWN + kv, gv)):
-            gr1[at_row] = t[:ROWS]
-            gr2[at_row] = t[ROWS:]
-            total = jnp.sum(t, axis=0, keepdims=True) + jnp.sum(
-                gkv_in[at_row], axis=0, keepdims=True
-            )
-            totals.append((Q_OWN + at_row, total))
+        for row, t in ((kv, gk * SCALE), (KV_OWN + kv, gv)):
+            for part, out in enumerate((r1s, r1x, r2s, r2x)):
+                out[row] = t[part * HALF : (part + 1) * HALF]
+            total = jnp.sum(t, axis=0, keepdims=True) + kv_sums[row : row + 1, :]
+            totals.append((Q_OWN + row, total))
     pad = SUM_ROWS - len(totals)
     totals = [t for _, t in sorted(totals, key=lambda t: t[0])] + [jnp.zeros((pad, HEAD_SIZE), F32)]
     sums[...] = jnp.broadcast_to(jnp.concatenate(totals, axis=0)[None], sums.shape)
 
 
-def cross_kernel(at, kv1, kv2, out):
-    out[0] = kv1[1]
-    out[1] = kv2[1]
-
-
-def kv_kernel(at, gkv, r1, r2, same, other):
-    for i in range(2 * KV_OWN):
-        same[i, :HALF] = (gkv[i, :HALF] + r1[i, :HALF]).astype(BF16)
-        same[i, HALF:] = (gkv[i, HALF:ROWS] + r2[i, :HALF]).astype(BF16)
-        other[i, :HALF] = (gkv[i, ROWS : ROWS + HALF] + r1[i, HALF:]).astype(BF16)
-        other[i, HALF:] = (gkv[i, ROWS + HALF :] + r2[i, HALF:]).astype(BF16)
+def cross_kernel(at, far, out):
+    out[...] = far[1]
 
 
 def join_q_kernel(at, same, other, out):
@@ -213,14 +204,15 @@
             out[:, pl.ds(base + h * HEAD_SIZE, HEAD_SIZE)] = part[h]
 
 
-def join_kv_kernel(at, same, other, out_k, out_v):
+def join_kv_kernel(at, same, other, r1s, r1x, r2s, r2x, out_k, out_v):
     core = at[0] % 2
-    for part, side in ((same, core), (other, 1 - core)):
+    for near, first, second, side in ((same, r1s, r2s, core), (other, r1x, r2x, 1 - core)):
         base = pl.multiple_of(side * (KV_OWN * HEAD_SIZE), KV_OWN * HEAD_SIZE)
         for h in range(KV_OWN):
             cols = pl.ds(base + h * HEAD_SIZE, HEAD_SIZE)
-            out_k[:, cols] = part[h]
-            out_v[:, cols] = part[KV_OWN + h]
+            for out, i in ((out_k, h), (out_v, KV_OWN + h)):
+                out[:HALF, cols] = (near[i, :HALF] + first[i]).astype(BF16)
+                out[HALF:, cols] = (near[i, HALF:] + second[i]).astype(BF16)
 
 
 def join_sums_kernel(at, parts, out_q, out_k, out_v):
@@ -253,52 +245,51 @@
     blocks = lambda count, rows=ROWS, dtype=BF16: shape(count, rows, HEAD_SIZE, dtype=dtype)
 
     dp = lax.axis_size("dp")
-    own, send, kv1, kv2 = call(
+    own, send, kvz = call(
         prep_kernel,
-        [blocks(PACK), blocks(PACK)] + [shape(2, 2 * KV_OWN, HALF, HEAD_SIZE)] * 2,
+        [blocks(PACK), blocks(PACK), shape(2, 2, 2 * KV_OWN, HALF, HEAD_SIZE)],
         9,
         moved=4 << 20,
-        keep=2,
         vmem=60 << 20,
     )(at, q_in[0, 0], k_in[0, 0], v_in[0, 0], o_in[0, 0], g_in[0, 0], lse[0, 0], bq, bk, bv)
 
-    up = [(i + chips, i) for i in range(chips)]
-    down = [(i, i + chips) for i in range(chips)]
-    kv1 = held(swapped(kv1, "ctx", chips))
-    kv2 = held(lax.ppermute(kv2, "ctx", up))
+    far = held(swapped(kvz, "ctx", chips))
     recv = held(swapped(send, "ctx", 1))
     own = held(own)
 
-    gq, gkv = call(
+    gq, kv_same, kv_other, kv_sums = call(
         functools.partial(local_kernel, ctx_count=n),
-        [blocks(Q_OWN, 2 * ROWS, F32), blocks(2 * KV_OWN, 2 * ROWS, F32)],
+        [blocks(Q_OWN, 2 * ROWS, F32)]
+        + [blocks(2 * KV_OWN, ROWS, F32)] * 2
+        + [shape(2 * KV_OWN, HEAD_SIZE, dtype=F32)],
         2,
         flops=700_000_000,
         moved=3 << 20,
     )(at, own, recv)
-    gq, gkv = held(gq), held(gkv)
-    (cross,) = call(cross_kernel, [shape(2, 2 * KV_OWN, HALF, HEAD_SIZE)], 2)(at, kv1, kv2)
+
+    def before(x, bit, senders=range(n)):
+        pairs = []
+        for s in range(1, lax.axis_size("section")):
+            pairs += [(s * n + c, (s - 1) * n + (c ^ bit)) for c in senders]
+        return held(lax.ppermute(x, ("section", "ctx"), pairs))
+
+    kv_same, kv_other = before(kv_same, 0), before(kv_other, 1)
+    (cross,) = call(cross_kernel, [shape(2, 2 * KV_OWN, HALF, HEAD_SIZE)], 1)(at, far)
     cross = held(swapped(cross, "ctx", 1))
-    gq_same, gq_other, gr1, gr2, sums = call(
+    gq_same, gq_other, r1s, r1x, r2s, r2x, sums = call(
         functools.partial(remote_kernel, ctx_count=n),
         [blocks(Q_OWN)] * 2
-        + [blocks(2 * KV_OWN, ROWS, F32)] * 2
+        + [blocks(2 * KV_OWN, HALF, F32)] * 4
         + [shape(n * dp, SUM_ROWS, HEAD_SIZE, dtype=F32)],
-        7,
+        6,
         flops=700_000_000,
         moved=4 << 20,
-        keep=4,
-    )(at, own, recv, kv1, kv2, cross, gq, gkv)
-
-    r1 = held(swapped(gr1, "ctx", chips))
-    r2 = held(lax.ppermute(gr2, "ctx", down))
-
-    def before(x, bit):
-        pairs = []
-        for s in range(1, lax.axis_size("section")):
-            pairs += [(s * n + c, (s - 1) * n + (c ^ bit)) for c in range(n)]
-        return held(lax.ppermute(x, ("section", "ctx"), pairs))
-
+        keep=6,
+    )(at, own, recv, far, cross, held(gq), held(kv_sums))
+
+    r2s = before(r2s, chips, range(chips))
+    r2x = before(r2x, chips + 1, range(chips))
+    r1s, r1x = before(r1s, chips), before(r1x, chips + 1)
     gq_same, gq_other = before(gq_same, 0), before(gq_other, 1)
     sums = lax.all_to_all(sums, ("ctx", "dp"), 0, 0, tiled=True)
     sum_q, sum_k, sum_v = call(
@@ -311,14 +302,12 @@
         1,
         keep=False,
     )(at, held(sums.reshape(n, dp, SUM_ROWS, HEAD_SIZE)))
-    kv_same, kv_other = call(kv_kernel, [blocks(2 * KV_OWN)] * 2, 3, moved=2 << 20)(at, gkv, r1, r2)
-    kv_same, kv_other = before(kv_same, 0), before(kv_other, 1)
+    recv_k, recv_v = call(
+        join_kv_kernel, [shape(ROWS, KV_HEADS * HEAD_SIZE)] * 2, 6, moved=2 << 20, keep=False
+    )(at, kv_same, kv_other, r1s, r1x, r2s, r2x)
     (recv_q,) = call(
         join_q_kernel, [shape(ROWS, Q_HEADS * HEAD_SIZE)], 2, moved=1 << 20, keep=False
     )(at, gq_same, gq_other)
-    recv_k, recv_v = call(
-        join_kv_kernel, [shape(ROWS, KV_HEADS * HEAD_SIZE)] * 2, 2, moved=1 << 19, keep=False
-    )(at, kv_same, kv_other)
     return (recv_q[None, None], recv_k[None, None], recv_v[None, None], sum_q, sum_k, sum_v)
 
 

time: 109 us -> 110 us (level)
  the two profiles are of different devices: /device:TPU:83 before, /device:TPU:353 now
where the time goes in v1:
time: 110 us
  starting transfers between devices  67.9 us (62%)
  waiting for transfers between devices  30.7 us (28%)
  Pallas kernels  10.6 us (10%)
    ppermute x8, starting transfers between devices, before(): return held(lax.ppermute(x, ('section', 'ctx'), pairs))  38.5 us
    ppermute x8, waiting for transfers between devices, before(): return held(lax.ppermute(x, ('section', 'ctx'), pairs))  20.1 us
    ppermute x3, starting transfers between devices, swapped(): return lax.ppermute(value, axis, [(i, i ^ bit) for i in range(size)])  17.5 us
    all_to_all x1, starting transfers between devices, body(): sums = lax.all_to_all(sums, ('ctx', 'dp'), 0, 0, tiled=True)  11.9 us
    ppermute x3, waiting for transfers between devices, swapped(): return lax.ppermute(value, axis, [(i, i ^ bit) for i in range(size)])  10.6 us
    pallas_call x1, Pallas kernels, body(): call(functools.partial(remote_kernel, ctx_count=n), [blocks(Q_OWN)] * 2 +...  3.42 us
    pallas_call x1, Pallas kernels, body(): call(functools.partial(local_kernel, ctx_count=n), [blocks(Q_OWN, 2 * ROW...  2.7 us
  transfers between devices with their start and end apart: 12, of which 5 were waited for; matrix products, arithmetic and copies ran while one was open for 0% of the time, Pallas kernels for 4%

profile of v1, /device:TPU:353, one launch (start us, length us, event | category | flops | bytes accessed | tf_op | source)
XLA Modules:
  0.0 110.0 jit_solution(17412042519931399430)
XLA Ops:
  0.6 2.2 %shard_map.136 = (bf16[21,128,128]{2,1,0:T(8,128)(2,1)S(1)}, bf16[21,128,128]{2,1,0:T(8,128)(2,1)S(1)}, bf16[2,2,4,64,128]{4,3,2,1,0:T(8,128)(2,1)S(1)}) custom-call(s32[1]{0:T(128)} %bitcast.at, bf16[128,2048]{1,0:T(8,128)(2,1)} %bitcast.13, bf16[128,512]{1,0:T(8,128)(2,1)} %bitcast.16, bf16[128,512]{1,0:T(8,128)(2,1)} %bitcast.17, ...), custom_call_target="tpu_custom_call" | custom-call | bytes 4194304 | tf_op jit(solution)/shard_map/pallas_call | solution.py:248
  2.8 2.6 %collective-permute-start = (bf16[21,128,128]{2,1,0:T(8,128)(2,1)S(1)}, bf16[21,128,128]{2,1,0:T(8,128)(2,1)S(1)}, u32[]{:S(2)}, u32[]{:S(2)}) collective-permute-start(bf16[21,128,128]{2,1,0:T(8,128)(2,1)S(1)} %get-tuple-element.26), channel_id=1, source_target_pairs={{0,8},{8,0},{16,24},{24,16},{1,9},{9,1},{17,25},{25,17},{2,10},{10... | collective-permute-start | bytes 2064392 | tf_op jit(solution)/shard_map/ppermute | solution.py:238
  5.4 12.5 %collective-permute-start.1 = (bf16[2,2,4,64,128]{4,3,2,1,0:T(8,128)(2,1)S(1)}, bf16[2,2,4,64,128]{4,3,2,1,0:T(8,128)(2,1)S(1)}, u32[]{:S(2)}, u32[]{:S(2)}) collective-permute-start(bf16[2,2,4,64,128]{4,3,2,1,0:T(8,128)(2,1)S(1)} %get-tuple-element.27), channel_id=1, source_target_pairs={{0,16},{8,24},{16,0},{24,8},{1,17},{9,25},{17,1},{25,9},{2,18},{10... | collective-permute-start | bytes 786440 | tf_op jit(solution)/shard_map/ppermute | solution.py:238
  17.9 10.6 %collective-permute-done.1.far = bf16[2,2,4,64,128]{4,3,2,1,0:T(8,128)(2,1)S(1)} collective-permute-done((bf16[2,2,4,64,128]{4,3,2,1,0:T(8,128)(2,1)S(1)}, bf16[2,2,4,64,128]{4,3,2,1,0:T(8,128)(2,1)S(1)}, u32[]{:S(2)}, u32[]{:S(2)}) %collective-permute-start.1) | collective-permute-done | bytes 262176 | tf_op jit(solution)/shard_map/ppermute | solution.py:238
  28.5 2.4 %collective-permute-start.2 = (bf16[2,4,64,128]{3,2,1,0:T(8,128)(2,1)S(1)}, bf16[2,4,64,128]{3,2,1,0:T(8,128)(2,1)S(1)}, u32[]{:S(2)}, u32[]{:S(2)}) collective-permute-start(bf16[2,4,64,128]{3,2,1,0:T(8,128)(2,1)S(1)} %shard_map.137), channel_id=1, source_target_pairs={{0,8},{8,0},{16,24},{24,16},{1,9},{9,1},{17,25},{25,17},{2,10},{10... | collective-permute-start | bytes 393224 | tf_op jit(solution)/shard_map/ppermute | solution.py:238
  31.0 0.0 collective-permute-done.recv
  31.0 2.7 %shard_map.138 = (f32[8,256,128]{2,1,0:T(8,128)S(1)}, f32[4,128,128]{2,1,0:T(8,128)S(1)}, f32[4,128,128]{2,1,0:T(8,128)S(1)}, f32[4,128]{1,0:T(4,128)S(1)}) custom-call(s32[1]{0:T(128)} %bitcast.at, bf16[21,128,128]{2,1,0:T(8,128)(2,1)S(1)} %get-tuple-element.25.own, bf16[21,128,128]{2,1,0:T(8,128)(2,1)S(1)} %collective-permute-done.recv), custom_call_target="tpu_custom_call" | custom-call | flops 700000000 | bytes 3145728 | tf_op jit(solution)/shard_map/pallas_call | solution.py:260
  33.7 0.0 collective-permute-done.2.cross
  33.7 3.4 %shard_map.139 = (bf16[8,128,128]{2,1,0:T(8,128)(2,1)S(1)}, bf16[8,128,128]{2,1,0:T(8,128)(2,1)S(1)}, f32[4,64,128]{2,1,0:T(8,128)S(1)}, f32[4,64,128]{2,1,0:T(8...) custom-call(s32[1]{0:T(128)} %bitcast.at, ...), custom_call_target="tpu_custom_call" | custom-call | flops 700000000 | bytes 4194304 | tf_op jit(solution)/shard_map/pallas_call | solution.py:279
  37.1 11.9 %all-to-all-start = ((f32[32,16,128]{2,1,0:T(8,128)}), f32[32,16,128]{2,1,0:T(8,128)S(1)}, u32[]{:S(2)}, u32[]{:S(2)}) async-start(f32[32,16,128]{2,1,0:T(8,128)} %get-tuple-element.40), calls=%async_computation | async-start | bytes 524288 | tf_op jit(solution)/shard_map/all_to_all | solution.py:294
  49.0 1.9 %collective-permute-start.3 = (bf16[8,128,128]{2,1,0:T(8,128)(2,1)S(1)}, bf16[8,128,128]{2,1,0:T(8,128)(2,1)S(1)}, u32[]{:S(2)}, u32[]{:S(2)}) collective-permute-start(bf16[8,128,128]{2,1,0:T(8,128)(2,1)S(1)} %get-tuple-element.30), channel_id=1, source_target_pairs={{32,0},{40,8},{48,16},{56,24},{64,32},{72,40},{80,48},{88,56},{96,... | collective-permute-start | bytes 786440 | tf_op jit(solution)/shard_map/ppermute | solution.py:274
  50.9 3.0 %collective-permute-start.4 = (bf16[8,128,128]{2,1,0:T(8,128)(2,1)S(1)}, bf16[8,128,128]{2,1,0:T(8,128)(2,1)S(1)}, u32[]{:S(2)}, u32[]{:S(2)}) collective-permute-start(bf16[8,128,128]{2,1,0:T(8,128)(2,1)S(1)} %get-tuple-element.31), channel_id=1, source_target_pairs={{32,8},{40,0},{48,24},{56,16},{64,40},{72,32},{80,56},{88,48},{96,... | collective-permute-start | bytes 786440 | tf_op jit(solution)/shard_map/ppermute | solution.py:274
  53.9 9.0 %collective-permute-start.7 = (f32[4,64,128]{2,1,0:T(8,128)S(1)}, f32[4,64,128]{2,1,0:T(8,128)S(1)}, u32[]{:S(2)}, u32[]{:S(2)}) collective-permute-start(f32[4,64,128]{2,1,0:T(8,128)S(1)} %get-tuple-element.34), channel_id=1, source_target_pairs={{32,16},{40,24},{48,0},{56,8},{64,48},{72,56},{80,32},{88,40},{96,... | collective-permute-start | bytes 393224 | tf_op jit(solution)/shard_map/ppermute | solution.py:274
  62.9 2.9 %collective-permute-start.5 = (f32[4,128,128]{2,1,0:T(8,128)S(1)}, f32[4,128,128]{2,1,0:T(8,128)S(1)}, u32[]{:S(2)}, u32[]{:S(2)}) collective-permute-start(f32[4,128,128]{2,1,0:T(8,128)S(1)} %get-tuple-element.32), channel_id=1, source_target_pairs={{32,0},{40,8},{48,16},{56,24},{64,32},{72,40},{80,48},{88,56},{96,... | collective-permute-start | bytes 786440 | tf_op jit(solution)/shard_map/ppermute | solution.py:274
  65.8 2.0 %collective-permute-start.6 = (f32[4,128,128]{2,1,0:T(8,128)S(1)}, f32[4,128,128]{2,1,0:T(8,128)S(1)}, u32[]{:S(2)}, u32[]{:S(2)}) collective-permute-start(f32[4,128,128]{2,1,0:T(8,128)S(1)} %get-tuple-element.33), channel_id=1, source_target_pairs={{32,8},{40,0},{48,24},{56,16},{64,40},{72,32},{80,56},{88,48},{96,... | collective-permute-start | bytes 786440 | tf_op jit(solution)/shard_map/ppermute | solution.py:274
  67.7 1.2 %collective-permute-done.7.r1s = f32[4,64,128]{2,1,0:T(8,128)S(1)} collective-permute-done((f32[4,64,128]{2,1,0:T(8,128)S(1)}, f32[4,64,128]{2,1,0:T(8,128)S(1)}, u32[]{:S(2)}, u32[]{:S(2)}) %collective-permute-start.7) | collective-permute-done | bytes 131104 | tf_op jit(solution)/shard_map/ppermute | solution.py:274
  69.0 14.5 %collective-permute-start.8 = (f32[4,64,128]{2,1,0:T(8,128)S(1)}, f32[4,64,128]{2,1,0:T(8,128)S(1)}, u32[]{:S(2)}, u32[]{:S(2)}) collective-permute-start(f32[4,64,128]{2,1,0:T(8,128)S(1)} %get-tuple-element.35), channel_id=1, source_target_pairs={{32,24},{40,16},{48,8},{56,0},{64,56},{72,48},{80,40},{88,32},{96,... | collective-permute-start | bytes 393224 | tf_op jit(solution)/shard_map/ppermute | solution.py:274
  83.4 0.0 collective-permute-done.3.same
  83.4 4.0 %collective-permute-start.9 = (f32[4,64,128]{2,1,0:T(8,128)S(1)}, f32[4,64,128]{2,1,0:T(8,128)S(1)}, u32[]{:S(2)}, u32[]{:S(2)}) collective-permute-start(f32[4,64,128]{2,1,0:T(8,128)S(1)} %get-tuple-element.36), channel_id=1, source_target_pairs={{32,16},{40,24},{64,48},{72,56},{96,80},{104,88},{128,112},{136,12... | collective-permute-start | bytes 393224 | tf_op jit(solution)/shard_map/ppermute | solution.py:274
  87.5 0.0 collective-permute-done.4.other
  87.5 1.3 %collective-permute-start.10 = (f32[4,64,128]{2,1,0:T(8,128)S(1)}, f32[4,64,128]{2,1,0:T(8,128)S(1)}, u32[]{:S(2)}, u32[]{:S(2)}) collective-permute-start(f32[4,64,128]{2,1,0:T(8,128)S(1)} %get-tuple-element.37), channel_id=1, source_target_pairs={{32,24},{40,16},{64,56},{72,48},{96,88},{104,80},{128,120},{136,11... | collective-permute-start | bytes 393224 | tf_op jit(solution)/shard_map/ppermute | solution.py:274
  88.8 0.9 shard_map.140
  89.7 2.1 %collective-permute-done.8.r1x = f32[4,64,128]{2,1,0:T(8,128)S(1)} collective-permute-done((f32[4,64,128]{2,1,0:T(8,128)S(1)}, f32[4,64,128]{2,1,0:T(8,128)S(1)}, u32[]{:S(2)}, u32[]{:S(2)}) %collective-permute-start.8) | collective-permute-done | bytes 131104 | tf_op jit(solution)/shard_map/ppermute | solution.py:274
  91.8 13.9 %collective-permute-done.9.r2s = f32[4,64,128]{2,1,0:T(8,128)S(1)} collective-permute-done((f32[4,64,128]{2,1,0:T(8,128)S(1)}, f32[4,64,128]{2,1,0:T(8,128)S(1)}, u32[]{:S(2)}, u32[]{:S(2)}) %collective-permute-start.9) | collective-permute-done | bytes 131104 | tf_op jit(solution)/shard_map/ppermute | solution.py:274
  105.8 2.8 %collective-permute-done.10.r2x = f32[4,64,128]{2,1,0:T(8,128)S(1)} collective-permute-done((f32[4,64,128]{2,1,0:T(8,128)S(1)}, f32[4,64,128]{2,1,0:T(8,128)S(1)}, u32[]{:S(2)}, u32[]{:S(2)}) %collective-permute-start.10) | collective-permute-done | bytes 131104 | tf_op jit(solution)/shard_map/ppermute | solution.py:274
  108.6 0.0 collective-permute-done.5.same
  108.6 0.0 collective-permute-done.6.other
  108.6 0.8 shard_map.141
  109.3 0.0 all-to-all-done
  109.3 0.6 shard_map.142
  (1 shorter events, 0.0 us)
Async XLA Ops:
  2.8 28.1 %collective-permute-start = (bf16[21,128,128]{2,1,0:T(8,128)(2,1)S(1)}, bf16[21,128,128]{2,1,0:T(8,128)(2,1)S(1)}, u32[]{:S(2)}, u32[]{:S(2)}) collective-permute-start(bf16[21,128,128]{2,1,0:T(8,128)(2,1)S(1)} %get-tuple-element.26), channel_id=1, source_target_pairs={{0,8},{8,0},{16,24},{24,16},{1,9},{9,1},{17,25},{25,17},{2,10},{10... | collective-permute-start | bytes 2064392 | tf_op jit(solution)/shard_map/ppermute | solution.py:238
  5.4 23.1 %collective-permute-start.1 = (bf16[2,2,4,64,128]{4,3,2,1,0:T(8,128)(2,1)S(1)}, bf16[2,2,4,64,128]{4,3,2,1,0:T(8,128)(2,1)S(1)}, u32[]{:S(2)}, u32[]{:S(2)}) collective-permute-start(bf16[2,2,4,64,128]{4,3,2,1,0:T(8,128)(2,1)S(1)} %get-tuple-element.27), channel_id=1, source_target_pairs={{0,16},{8,24},{16,0},{24,8},{1,17},{9,25},{17,1},{25,9},{2,18},{10... | collective-permute-start | bytes 786440 | tf_op jit(solution)/shard_map/ppermute | solution.py:238
  28.5 5.1 %collective-permute-start.2 = (bf16[2,4,64,128]{3,2,1,0:T(8,128)(2,1)S(1)}, bf16[2,4,64,128]{3,2,1,0:T(8,128)(2,1)S(1)}, u32[]{:S(2)}, u32[]{:S(2)}) collective-permute-start(bf16[2,4,64,128]{3,2,1,0:T(8,128)(2,1)S(1)} %shard_map.137), channel_id=1, source_target_pairs={{0,8},{8,0},{16,24},{24,16},{1,9},{9,1},{17,25},{25,17},{2,10},{10... | collective-permute-start | bytes 393224 | tf_op jit(solution)/shard_map/ppermute | solution.py:238
  37.1 72.2 %all-to-all-start = ((f32[32,16,128]{2,1,0:T(8,128)}), f32[32,16,128]{2,1,0:T(8,128)S(1)}, u32[]{:S(2)}, u32[]{:S(2)}) async-start(f32[32,16,128]{2,1,0:T(8,128)} %get-tuple-element.40), calls=%async_computation | async-start | bytes 524288 | tf_op jit(solution)/shard_map/all_to_all | solution.py:294
  49.0 34.5 %collective-permute-start.3 = (bf16[8,128,128]{2,1,0:T(8,128)(2,1)S(1)}, bf16[8,128,128]{2,1,0:T(8,128)(2,1)S(1)}, u32[]{:S(2)}, u32[]{:S(2)}) collective-permute-start(bf16[8,128,128]{2,1,0:T(8,128)(2,1)S(1)} %get-tuple-element.30), channel_id=1, source_target_pairs={{32,0},{40,8},{48,16},{56,24},{64,32},{72,40},{80,48},{88,56},{96,... | collective-permute-start | bytes 786440 | tf_op jit(solution)/shard_map/ppermute | solution.py:274
  50.9 36.6 %collective-permute-start.4 = (bf16[8,128,128]{2,1,0:T(8,128)(2,1)S(1)}, bf16[8,128,128]{2,1,0:T(8,128)(2,1)S(1)}, u32[]{:S(2)}, u32[]{:S(2)}) collective-permute-start(bf16[8,128,128]{2,1,0:T(8,128)(2,1)S(1)} %get-tuple-element.31), channel_id=1, source_target_pairs={{32,8},{40,0},{48,24},{56,16},{64,40},{72,32},{80,56},{88,48},{96,... | collective-permute-start | bytes 786440 | tf_op jit(solution)/shard_map/ppermute | solution.py:274
  53.9 15.0 %collective-permute-start.7 = (f32[4,64,128]{2,1,0:T(8,128)S(1)}, f32[4,64,128]{2,1,0:T(8,128)S(1)}, u32[]{:S(2)}, u32[]{:S(2)}) collective-permute-start(f32[4,64,128]{2,1,0:T(8,128)S(1)} %get-tuple-element.34), channel_id=1, source_target_pairs={{32,16},{40,24},{48,0},{56,8},{64,48},{72,56},{80,32},{88,40},{96,... | collective-permute-start | bytes 393224 | tf_op jit(solution)/shard_map/ppermute | solution.py:274
  62.9 45.7 %collective-permute-start.5 = (f32[4,128,128]{2,1,0:T(8,128)S(1)}, f32[4,128,128]{2,1,0:T(8,128)S(1)}, u32[]{:S(2)}, u32[]{:S(2)}) collective-permute-start(f32[4,128,128]{2,1,0:T(8,128)S(1)} %get-tuple-element.32), channel_id=1, source_target_pairs={{32,0},{40,8},{48,16},{56,24},{64,32},{72,40},{80,48},{88,56},{96,... | collective-permute-start | bytes 786440 | tf_op jit(solution)/shard_map/ppermute | solution.py:274
  65.8 42.8 %collective-permute-start.6 = (f32[4,128,128]{2,1,0:T(8,128)S(1)}, f32[4,128,128]{2,1,0:T(8,128)S(1)}, u32[]{:S(2)}, u32[]{:S(2)}) collective-permute-start(f32[4,128,128]{2,1,0:T(8,128)S(1)} %get-tuple-element.33), channel_id=1, source_target_pairs={{32,8},{40,0},{48,24},{56,16},{64,40},{72,32},{80,56},{88,48},{96,... | collective-permute-start | bytes 786440 | tf_op jit(solution)/shard_map/ppermute | solution.py:274
  69.0 22.9 %collective-permute-start.8 = (f32[4,64,128]{2,1,0:T(8,128)S(1)}, f32[4,64,128]{2,1,0:T(8,128)S(1)}, u32[]{:S(2)}, u32[]{:S(2)}) collective-permute-start(f32[4,64,128]{2,1,0:T(8,128)S(1)} %get-tuple-element.35), channel_id=1, source_target_pairs={{32,24},{40,16},{48,8},{56,0},{64,56},{72,48},{80,40},{88,32},{96,... | collective-permute-start | bytes 393224 | tf_op jit(solution)/shard_map/ppermute | solution.py:274
  83.4 22.3 %collective-permute-start.9 = (f32[4,64,128]{2,1,0:T(8,128)S(1)}, f32[4,64,128]{2,1,0:T(8,128)S(1)}, u32[]{:S(2)}, u32[]{:S(2)}) collective-permute-start(f32[4,64,128]{2,1,0:T(8,128)S(1)} %get-tuple-element.36), channel_id=1, source_target_pairs={{32,16},{40,24},{64,48},{72,56},{96,80},{104,88},{128,112},{136,12... | collective-permute-start | bytes 393224 | tf_op jit(solution)/shard_map/ppermute | solution.py:274
  87.5 21.1 %collective-permute-start.10 = (f32[4,64,128]{2,1,0:T(8,128)S(1)}, f32[4,64,128]{2,1,0:T(8,128)S(1)}, u32[]{:S(2)}, u32[]{:S(2)}) collective-permute-start(f32[4,64,128]{2,1,0:T(8,128)S(1)} %get-tuple-element.37), channel_id=1, source_target_pairs={{32,24},{40,16},{64,56},{72,48},{96,88},{104,80},{128,120},{136,11... | collective-permute-start | bytes 393224 | tf_op jit(solution)/shard_map/ppermute | solution.py:274

commit v2 on v1

--- a/solution.py
+++ b/solution.py
@@ -189,7 +189,7 @@
             totals.append((Q_OWN + row, total))
     pad = SUM_ROWS - len(totals)
     totals = [t for _, t in sorted(totals, key=lambda t: t[0])] + [jnp.zeros((pad, HEAD_SIZE), F32)]
-    sums[...] = jnp.broadcast_to(jnp.concatenate(totals, axis=0)[None], sums.shape)
+    sums[...] = jnp.concatenate(totals, axis=0)
 
 
 def cross_kernel(at, far, out):
@@ -215,22 +215,30 @@
                 out[HALF:, cols] = (near[i, HALF:] + second[i]).astype(BF16)
 
 
-def join_sums_kernel(at, parts, out_q, out_k, out_v):
-    ctx_count, dp_count = parts.shape[:2]
-    for core in range(2):
-        total = None
-        for c in range(core, ctx_count, 2):
-            for r in range(dp_count):
-                total = parts[c, r] if total is None else total + parts[c, r]
+def pair_sums_kernel(at, mine, theirs, out):
+    out[...] = jnp.broadcast_to((mine[...] + theirs[...])[None], out.shape)
+
+
+def replica_sums_kernel(at, parts, out):
+    total = parts[0]
+    for r in range(1, parts.shape[0]):
+        total = total + parts[r]
+    out[...] = total
+
+
+def join_sums_kernel(at, same, other, out_q, out_k, out_v):
+    core = at[0] % 2
+    for part, side in ((same, core), (other, 1 - core)):
+        base = pl.multiple_of(side * (Q_OWN * HEAD_SIZE), Q_OWN * HEAD_SIZE)
+        kv_base = pl.multiple_of(side * (KV_OWN * HEAD_SIZE), KV_OWN * HEAD_SIZE)
         for h in range(Q_OWN):
-            at_col = (core * Q_OWN + h) * HEAD_SIZE
-            out_q[:, at_col : at_col + HEAD_SIZE] = total[h : h + 1]
+            out_q[:, pl.ds(base + h * HEAD_SIZE, HEAD_SIZE)] = part[h : h + 1, :]
         for h in range(KV_OWN):
-            at_col = (core * KV_OWN + h) * HEAD_SIZE
+            cols = pl.ds(kv_base + h * HEAD_SIZE, HEAD_SIZE)
             row = Q_OWN + h
-            out_k[:, at_col : at_col + HEAD_SIZE] = total[row : row + 1]
+            out_k[:, cols] = part[row : row + 1, :]
             row += KV_OWN
-            out_v[:, at_col : at_col + HEAD_SIZE] = total[row : row + 1]
+            out_v[:, cols] = part[row : row + 1, :]
 
 
 def swapped(value, axis, bit):
@@ -280,18 +288,22 @@
         functools.partial(remote_kernel, ctx_count=n),
         [blocks(Q_OWN)] * 2
         + [blocks(2 * KV_OWN, HALF, F32)] * 4
-        + [shape(n * dp, SUM_ROWS, HEAD_SIZE, dtype=F32)],
+        + [shape(SUM_ROWS, HEAD_SIZE, dtype=F32)],
         6,
         flops=700_000_000,
         moved=4 << 20,
-        keep=6,
     )(at, own, recv, far, cross, held(gq), held(kv_sums))
 
     r2s = before(r2s, chips, range(chips))
     r2x = before(r2x, chips + 1, range(chips))
     r1s, r1x = before(r1s, chips), before(r1x, chips + 1)
     gq_same, gq_other = before(gq_same, 0), before(gq_other, 1)
-    sums = lax.all_to_all(sums, ("ctx", "dp"), 0, 0, tiled=True)
+    far_sums = held(swapped(sums, "ctx", chips))
+    (copies,) = call(
+        pair_sums_kernel, [shape(dp, SUM_ROWS, HEAD_SIZE, dtype=F32)], 2, keep=False
+    )(at, held(sums), far_sums)
+    copies = held(lax.all_to_all(copies, "dp", 0, 0, tiled=True))
+    (sums,) = call(replica_sums_kernel, [shape(SUM_ROWS, HEAD_SIZE, dtype=F32)], 1)(at, copies)
     sum_q, sum_k, sum_v = call(
         join_sums_kernel,
         [
@@ -299,9 +311,9 @@
             shape(1, KV_HEADS * HEAD_SIZE, dtype=F32),
             shape(1, KV_HEADS * HEAD_SIZE, dtype=F32),
         ],
-        1,
+        2,
         keep=False,
-    )(at, held(sums.reshape(n, dp, SUM_ROWS, HEAD_SIZE)))
+    )(at, held(sums), held(swapped(sums, "ctx", 1)))
     recv_k, recv_v = call(
         join_kv_kernel, [shape(ROWS, KV_HEADS * HEAD_SIZE)] * 2, 6, moved=2 << 20, keep=False
     )(at, kv_same, kv_other, r1s, r1x, r2s, r2x)

time: 110 us -> 116 us (1.055)
  the two profiles are of different devices: /device:TPU:353 before, /device:TPU:433 now
where the time goes in v2:
time: 116 us; the launch traced here: 115 us
  starting transfers between devices  58.9 us (51%)
  waiting for transfers between devices  32.2 us (28%)
  blocking collectives  13.5 us (12%)
  Pallas kernels  9.9 us (9%)
    ppermute x8, starting transfers between devices, before(): return held(lax.ppermute(x, ('section', 'ctx'), pairs))  38 us
    ppermute x5, starting transfers between devices, swapped(): return lax.ppermute(value, axis, [(i, i ^ bit) for i in range(size)])  20.8 us
    ppermute x8, waiting for transfers between devices, before(): return held(lax.ppermute(x, ('section', 'ctx'), pairs))  18.8 us
    all_to_all x1, blocking collectives, body(): copies = held(lax.all_to_all(copies, 'dp', 0, 0, tiled=True))  13.5 us
    ppermute x5, waiting for transfers between devices, swapped(): return lax.ppermute(value, axis, [(i, i ^ bit) for i in range(size)])  13.4 us
    pallas_call x1, Pallas kernels, body(): call(functools.partial(remote_kernel, ctx_count=n), [blocks(Q_OWN)] * 2 +...  2.7 us
    pallas_call x1, Pallas kernels, body(): call(functools.partial(local_kernel, ctx_count=n), [blocks(Q_OWN, 2 * ROW...  2.67 us
  transfers between devices with their start and end apart: 13, of which 5 were waited for; matrix products, arithmetic and copies ran while one was open for 0% of the time, Pallas kernels for 4%

profile of v2, /device:TPU:433, one launch (start us, length us, event | category | flops | bytes accessed | tf_op | source)
XLA Modules:
  0.0 115.3 jit_solution(8298580728954006919)
XLA Ops:
  0.6 2.2 %shard_map.136 = (bf16[21,128,128]{2,1,0:T(8,128)(2,1)S(1)}, bf16[21,128,128]{2,1,0:T(8,128)(2,1)S(1)}, bf16[2,2,4,64,128]{4,3,2,1,0:T(8,128)(2,1)S(1)}) custom-call(s32[1]{0:T(128)} %bitcast.at, bf16[128,2048]{1,0:T(8,128)(2,1)} %bitcast.11, bf16[128,512]{1,0:T(8,128)(2,1)} %bitcast.14, bf16[128,512]{1,0:T(8,128)(2,1)} %bitcast.15, ...), custom_call_target="tpu_custom_call" | custom-call | bytes 4194304 | tf_op jit(solution)/shard_map/pallas_call | solution.py:256
  2.8 2.6 %collective-permute-start = (bf16[21,128,128]{2,1,0:T(8,128)(2,1)S(1)}, bf16[21,128,128]{2,1,0:T(8,128)(2,1)S(1)}, u32[]{:S(2)}, u32[]{:S(2)}) collective-permute-start(bf16[21,128,128]{2,1,0:T(8,128)(2,1)S(1)} %get-tuple-element.26), channel_id=1, source_target_pairs={{0,8},{8,0},{16,24},{24,16},{1,9},{9,1},{17,25},{25,17},{2,10},{10... | collective-permute-start | bytes 2064392 | tf_op jit(solution)/shard_map/ppermute | solution.py:246
  5.4 11.6 %collective-permute-start.1 = (bf16[2,2,4,64,128]{4,3,2,1,0:T(8,128)(2,1)S(1)}, bf16[2,2,4,64,128]{4,3,2,1,0:T(8,128)(2,1)S(1)}, u32[]{:S(2)}, u32[]{:S(2)}) collective-permute-start(bf16[2,2,4,64,128]{4,3,2,1,0:T(8,128)(2,1)S(1)} %get-tuple-element.27), channel_id=1, source_target_pairs={{0,16},{8,24},{16,0},{24,8},{1,17},{9,25},{17,1},{25,9},{2,18},{10... | collective-permute-start | bytes 786440 | tf_op jit(solution)/shard_map/ppermute | solution.py:246
  17.0 12.3 %collective-permute-done.1.far = bf16[2,2,4,64,128]{4,3,2,1,0:T(8,128)(2,1)S(1)} collective-permute-done((bf16[2,2,4,64,128]{4,3,2,1,0:T(8,128)(2,1)S(1)}, bf16[2,2,4,64,128]{4,3,2,1,0:T(8,128)(2,1)S(1)}, u32[]{:S(2)}, u32[]{:S(2)}) %collective-permute-start.1) | collective-permute-done | bytes 262176 | tf_op jit(solution)/shard_map/ppermute | solution.py:246
  29.3 2.5 %collective-permute-start.2 = (bf16[2,4,64,128]{3,2,1,0:T(8,128)(2,1)S(1)}, bf16[2,4,64,128]{3,2,1,0:T(8,128)(2,1)S(1)}, u32[]{:S(2)}, u32[]{:S(2)}) collective-permute-start(bf16[2,4,64,128]{3,2,1,0:T(8,128)(2,1)S(1)} %shard_map.137), channel_id=1, source_target_pairs={{0,8},{8,0},{16,24},{24,16},{1,9},{9,1},{17,25},{25,17},{2,10},{10... | collective-permute-start | bytes 393224 | tf_op jit(solution)/shard_map/ppermute | solution.py:246
  31.8 0.0 collective-permute-done.recv
  31.8 2.7 %shard_map.138 = (f32[8,256,128]{2,1,0:T(8,128)S(1)}, f32[4,128,128]{2,1,0:T(8,128)S(1)}, f32[4,128,128]{2,1,0:T(8,128)S(1)}, f32[4,128]{1,0:T(4,128)S(1)}) custom-call(s32[1]{0:T(128)} %bitcast.at, bf16[21,128,128]{2,1,0:T(8,128)(2,1)S(1)} %get-tuple-element.25.own, bf16[21,128,128]{2,1,0:T(8,128)(2,1)S(1)} %collective-permute-done.recv), custom_call_target="tpu_custom_call" | custom-call | flops 700000000 | bytes 3145728 | tf_op jit(solution)/shard_map/pallas_call | solution.py:268
  34.5 0.0 collective-permute-done.2.cross
  34.5 2.7 %shard_map.139 = (bf16[8,128,128]{2,1,0:T(8,128)(2,1)S(1)}, bf16[8,128,128]{2,1,0:T(8,128)(2,1)S(1)}, f32[4,64,128]{2,1,0:T(8,128)S(1)}, f32[4,64,128]{2,1,0:T(8...) custom-call(s32[1]{0:T(128)} %bitcast.at, ...), custom_call_target="tpu_custom_call" | custom-call | flops 700000000 | bytes 4194304 | tf_op jit(solution)/shard_map/pallas_call | solution.py:287
  37.2 1.9 %collective-permute-start.3 = (bf16[8,128,128]{2,1,0:T(8,128)(2,1)S(1)}, bf16[8,128,128]{2,1,0:T(8,128)(2,1)S(1)}, u32[]{:S(2)}, u32[]{:S(2)}) collective-permute-start(bf16[8,128,128]{2,1,0:T(8,128)(2,1)S(1)} %get-tuple-element.30), channel_id=1, source_target_pairs={{32,0},{40,8},{48,16},{56,24},{64,32},{72,40},{80,48},{88,56},{96,... | collective-permute-start | bytes 786440 | tf_op jit(solution)/shard_map/ppermute | solution.py:282
  39.2 1.9 %collective-permute-start.4 = (bf16[8,128,128]{2,1,0:T(8,128)(2,1)S(1)}, bf16[8,128,128]{2,1,0:T(8,128)(2,1)S(1)}, u32[]{:S(2)}, u32[]{:S(2)}) collective-permute-start(bf16[8,128,128]{2,1,0:T(8,128)(2,1)S(1)} %get-tuple-element.31), channel_id=1, source_target_pairs={{32,8},{40,0},{48,24},{56,16},{64,40},{72,32},{80,56},{88,48},{96,... | collective-permute-start | bytes 786440 | tf_op jit(solution)/shard_map/ppermute | solution.py:282
  41.1 4.3 %collective-permute-start.7 = (f32[4,64,128]{2,1,0:T(8,128)S(1)}, f32[4,64,128]{2,1,0:T(8,128)S(1)}, u32[]{:S(2)}, u32[]{:S(2)}) collective-permute-start(f32[4,64,128]{2,1,0:T(8,128)S(1)} %get-tuple-element.34), channel_id=1, source_target_pairs={{32,16},{40,24},{48,0},{56,8},{64,48},{72,56},{80,32},{88,40},{96,... | collective-permute-start | bytes 393224 | tf_op jit(solution)/shard_map/ppermute | solution.py:282
  45.4 2.2 %collective-permute-start.11 = (f32[16,128]{1,0:T(8,128)S(1)}, f32[16,128]{1,0:T(8,128)S(1)}, u32[]{:S(2)}, u32[]{:S(2)}) collective-permute-start(f32[16,128]{1,0:T(8,128)S(1)} %get-tuple-element.40.mine), channel_id=1, source_target_pairs={{0,16},{8,24},{16,0},{24,8},{1,17},{9,25},{17,1},{25,9},{2,18},{10... | collective-permute-start | bytes 24584 | tf_op jit(solution)/shard_map/ppermute | solution.py:246
  47.6 7.2 %collective-permute-start.5 = (f32[4,128,128]{2,1,0:T(8,128)S(1)}, f32[4,128,128]{2,1,0:T(8,128)S(1)}, u32[]{:S(2)}, u32[]{:S(2)}) collective-permute-start(f32[4,128,128]{2,1,0:T(8,128)S(1)} %get-tuple-element.32), channel_id=1, source_target_pairs={{32,0},{40,8},{48,16},{56,24},{64,32},{72,40},{80,48},{88,56},{96,... | collective-permute-start | bytes 786440 | tf_op jit(solution)/shard_map/ppermute | solution.py:282
  54.8 0.0 collective-permute-done.11.theirs
  54.8 12.1 %collective-permute-start.6 = (f32[4,128,128]{2,1,0:T(8,128)S(1)}, f32[4,128,128]{2,1,0:T(8,128)S(1)}, u32[]{:S(2)}, u32[]{:S(2)}) collective-permute-start(f32[4,128,128]{2,1,0:T(8,128)S(1)} %get-tuple-element.33), channel_id=1, source_target_pairs={{32,8},{40,0},{48,24},{56,16},{64,40},{72,32},{80,56},{88,48},{96,... | collective-permute-start | bytes 786440 | tf_op jit(solution)/shard_map/ppermute | solution.py:282
  66.9 13.5 %all_to_all.5.parts = f32[8,16,128]{2,1,0:T(8,128)S(1)} all-to-all(f32[8,16,128]{2,1,0:T(8,128)S(1)} %shard_map.142), channel_id=1, replica_groups=mesh['section'=32,'ctx'=4,'dp'=8] {'dp'}, dimensions={0} | all-to-all | bytes 131072 | tf_op jit(solution)/shard_map/all_to_all | solution.py:305
  80.5 0.0 collective-permute-done.7.r1s
  80.5 1.9 %collective-permute-start.12 = (f32[16,128]{1,0:T(8,128)S(1)}, f32[16,128]{1,0:T(8,128)S(1)}, u32[]{:S(2)}, u32[]{:S(2)}) collective-permute-start(f32[16,128]{1,0:T(8,128)S(1)} %shard_map.143.same), channel_id=1, source_target_pairs={{0,8},{8,0},{16,24},{24,16},{1,9},{9,1},{17,25},{25,17},{2,10},{10... | collective-permute-start | bytes 24584 | tf_op jit(solution)/shard_map/ppermute | solution.py:246
  82.4 1.1 collective-permute-done.12.other
  83.5 7.4 %collective-permute-start.8 = (f32[4,64,128]{2,1,0:T(8,128)S(1)}, f32[4,64,128]{2,1,0:T(8,128)S(1)}, u32[]{:S(2)}, u32[]{:S(2)}) collective-permute-start(f32[4,64,128]{2,1,0:T(8,128)S(1)} %get-tuple-element.35), channel_id=1, source_target_pairs={{32,24},{40,16},{48,8},{56,0},{64,56},{72,48},{80,40},{88,32},{96,... | collective-permute-start | bytes 393224 | tf_op jit(solution)/shard_map/ppermute | solution.py:282
  91.0 0.0 collective-permute-done.3.same
  91.0 1.7 %collective-permute-start.9 = (f32[4,64,128]{2,1,0:T(8,128)S(1)}, f32[4,64,128]{2,1,0:T(8,128)S(1)}, u32[]{:S(2)}, u32[]{:S(2)}) collective-permute-start(f32[4,64,128]{2,1,0:T(8,128)S(1)} %get-tuple-element.36), channel_id=1, source_target_pairs={{32,16},{40,24},{64,48},{72,56},{96,80},{104,88},{128,112},{136,12... | collective-permute-start | bytes 393224 | tf_op jit(solution)/shard_map/ppermute | solution.py:282
  92.7 0.0 collective-permute-done.4.other
  92.7 1.5 %collective-permute-start.10 = (f32[4,64,128]{2,1,0:T(8,128)S(1)}, f32[4,64,128]{2,1,0:T(8,128)S(1)}, u32[]{:S(2)}, u32[]{:S(2)}) collective-permute-start(f32[4,64,128]{2,1,0:T(8,128)S(1)} %get-tuple-element.37), channel_id=1, source_target_pairs={{32,24},{40,16},{64,56},{72,48},{96,88},{104,80},{128,120},{136,11... | collective-permute-start | bytes 393224 | tf_op jit(solution)/shard_map/ppermute | solution.py:282
  94.2 0.6 shard_map.144
  94.8 0.9 shard_map.140
  95.8 13.1 %collective-permute-done.8.r1x = f32[4,64,128]{2,1,0:T(8,128)S(1)} collective-permute-done((f32[4,64,128]{2,1,0:T(8,128)S(1)}, f32[4,64,128]{2,1,0:T(8,128)S(1)}, u32[]{:S(2)}, u32[]{:S(2)}) %collective-permute-start.8) | collective-permute-done | bytes 131104 | tf_op jit(solution)/shard_map/ppermute | solution.py:282
  108.9 2.8 %collective-permute-done.9.r2s = f32[4,64,128]{2,1,0:T(8,128)S(1)} collective-permute-done((f32[4,64,128]{2,1,0:T(8,128)S(1)}, f32[4,64,128]{2,1,0:T(8,128)S(1)}, u32[]{:S(2)}, u32[]{:S(2)}) %collective-permute-start.9) | collective-permute-done | bytes 131104 | tf_op jit(solution)/shard_map/ppermute | solution.py:282
  111.7 2.8 %collective-permute-done.10.r2x = f32[4,64,128]{2,1,0:T(8,128)S(1)} collective-permute-done((f32[4,64,128]{2,1,0:T(8,128)S(1)}, f32[4,64,128]{2,1,0:T(8,128)S(1)}, u32[]{:S(2)}, u32[]{:S(2)}) %collective-permute-start.10) | collective-permute-done | bytes 131104 | tf_op jit(solution)/shard_map/ppermute | solution.py:282
  114.5 0.0 collective-permute-done.5.same
  114.5 0.0 collective-permute-done.6.other
  114.5 0.8 shard_map.141
  (3 shorter events, 0.0 us)
Async XLA Ops:
  2.8 29.0 %collective-permute-start = (bf16[21,128,128]{2,1,0:T(8,128)(2,1)S(1)}, bf16[21,128,128]{2,1,0:T(8,128)(2,1)S(1)}, u32[]{:S(2)}, u32[]{:S(2)}) collective-permute-start(bf16[21,128,128]{2,1,0:T(8,128)(2,1)S(1)} %get-tuple-element.26), channel_id=1, source_target_pairs={{0,8},{8,0},{16,24},{24,16},{1,9},{9,1},{17,25},{25,17},{2,10},{10... | collective-permute-start | bytes 2064392 | tf_op jit(solution)/shard_map/ppermute | solution.py:246
  5.4 23.9 %collective-permute-start.1 = (bf16[2,2,4,64,128]{4,3,2,1,0:T(8,128)(2,1)S(1)}, bf16[2,2,4,64,128]{4,3,2,1,0:T(8,128)(2,1)S(1)}, u32[]{:S(2)}, u32[]{:S(2)}) collective-permute-start(bf16[2,2,4,64,128]{4,3,2,1,0:T(8,128)(2,1)S(1)} %get-tuple-element.27), channel_id=1, source_target_pairs={{0,16},{8,24},{16,0},{24,8},{1,17},{9,25},{17,1},{25,9},{2,18},{10... | collective-permute-start | bytes 786440 | tf_op jit(solution)/shard_map/ppermute | solution.py:246
  29.3 5.2 %collective-permute-start.2 = (bf16[2,4,64,128]{3,2,1,0:T(8,128)(2,1)S(1)}, bf16[2,4,64,128]{3,2,1,0:T(8,128)(2,1)S(1)}, u32[]{:S(2)}, u32[]{:S(2)}) collective-permute-start(bf16[2,4,64,128]{3,2,1,0:T(8,128)(2,1)S(1)} %shard_map.137), channel_id=1, source_target_pairs={{0,8},{8,0},{16,24},{24,16},{1,9},{9,1},{17,25},{25,17},{2,10},{10... | collective-permute-start | bytes 393224 | tf_op jit(solution)/shard_map/ppermute | solution.py:246
  37.2 53.7 %collective-permute-start.3 = (bf16[8,128,128]{2,1,0:T(8,128)(2,1)S(1)}, bf16[8,128,128]{2,1,0:T(8,128)(2,1)S(1)}, u32[]{:S(2)}, u32[]{:S(2)}) collective-permute-start(bf16[8,128,128]{2,1,0:T(8,128)(2,1)S(1)} %get-tuple-element.30), channel_id=1, source_target_pairs={{32,0},{40,8},{48,16},{56,24},{64,32},{72,40},{80,48},{88,56},{96,... | collective-permute-start | bytes 786440 | tf_op jit(solution)/shard_map/ppermute | solution.py:282
  39.2 53.5 %collective-permute-start.4 = (bf16[8,128,128]{2,1,0:T(8,128)(2,1)S(1)}, bf16[8,128,128]{2,1,0:T(8,128)(2,1)S(1)}, u32[]{:S(2)}, u32[]{:S(2)}) collective-permute-start(bf16[8,128,128]{2,1,0:T(8,128)(2,1)S(1)} %get-tuple-element.31), channel_id=1, source_target_pairs={{32,8},{40,0},{48,24},{56,16},{64,40},{72,32},{80,56},{88,48},{96,... | collective-permute-start | bytes 786440 | tf_op jit(solution)/shard_map/ppermute | solution.py:282
  41.1 39.4 %collective-permute-start.7 = (f32[4,64,128]{2,1,0:T(8,128)S(1)}, f32[4,64,128]{2,1,0:T(8,128)S(1)}, u32[]{:S(2)}, u32[]{:S(2)}) collective-permute-start(f32[4,64,128]{2,1,0:T(8,128)S(1)} %get-tuple-element.34), channel_id=1, source_target_pairs={{32,16},{40,24},{48,0},{56,8},{64,48},{72,56},{80,32},{88,40},{96,... | collective-permute-start | bytes 393224 | tf_op jit(solution)/shard_map/ppermute | solution.py:282
  45.4 9.4 %collective-permute-start.11 = (f32[16,128]{1,0:T(8,128)S(1)}, f32[16,128]{1,0:T(8,128)S(1)}, u32[]{:S(2)}, u32[]{:S(2)}) collective-permute-start(f32[16,128]{1,0:T(8,128)S(1)} %get-tuple-element.40.mine), channel_id=1, source_target_pairs={{0,16},{8,24},{16,0},{24,8},{1,17},{9,25},{17,1},{25,9},{2,18},{10... | collective-permute-start | bytes 24584 | tf_op jit(solution)/shard_map/ppermute | solution.py:246
  47.6 66.9 %collective-permute-start.5 = (f32[4,128,128]{2,1,0:T(8,128)S(1)}, f32[4,128,128]{2,1,0:T(8,128)S(1)}, u32[]{:S(2)}, u32[]{:S(2)}) collective-permute-start(f32[4,128,128]{2,1,0:T(8,128)S(1)} %get-tuple-element.32), channel_id=1, source_target_pairs={{32,0},{40,8},{48,16},{56,24},{64,32},{72,40},{80,48},{88,56},{96,... | collective-permute-start | bytes 786440 | tf_op jit(solution)/shard_map/ppermute | solution.py:282
  54.8 59.7 %collective-permute-start.6 = (f32[4,128,128]{2,1,0:T(8,128)S(1)}, f32[4,128,128]{2,1,0:T(8,128)S(1)}, u32[]{:S(2)}, u32[]{:S(2)}) collective-permute-start(f32[4,128,128]{2,1,0:T(8,128)S(1)} %get-tuple-element.33), channel_id=1, source_target_pairs={{32,8},{40,0},{48,24},{56,16},{64,40},{72,32},{80,56},{88,48},{96,... | collective-permute-start | bytes 786440 | tf_op jit(solution)/shard_map/ppermute | solution.py:282
  80.5 3.1 %collective-permute-start.12 = (f32[16,128]{1,0:T(8,128)S(1)}, f32[16,128]{1,0:T(8,128)S(1)}, u32[]{:S(2)}, u32[]{:S(2)}) collective-permute-start(f32[16,128]{1,0:T(8,128)S(1)} %shard_map.143.same), channel_id=1, source_target_pairs={{0,8},{8,0},{16,24},{24,16},{1,9},{9,1},{17,25},{25,17},{2,10},{10... | collective-permute-start | bytes 24584 | tf_op jit(solution)/shard_map/ppermute | solution.py:246
  83.5 25.4 %collective-permute-start.8 = (f32[4,64,128]{2,1,0:T(8,128)S(1)}, f32[4,64,128]{2,1,0:T(8,128)S(1)}, u32[]{:S(2)}, u32[]{:S(2)}) collective-permute-start(f32[4,64,128]{2,1,0:T(8,128)S(1)} %get-tuple-element.35), channel_id=1, source_target_pairs={{32,24},{40,16},{48,8},{56,0},{64,56},{72,48},{80,40},{88,32},{96,... | collective-permute-start | bytes 393224 | tf_op jit(solution)/shard_map/ppermute | solution.py:282
  91.0 20.8 %collective-permute-start.9 = (f32[4,64,128]{2,1,0:T(8,128)S(1)}, f32[4,64,128]{2,1,0:T(8,128)S(1)}, u32[]{:S(2)}, u32[]{:S(2)}) collective-permute-start(f32[4,64,128]{2,1,0:T(8,128)S(1)} %get-tuple-element.36), channel_id=1, source_target_pairs={{32,16},{40,24},{64,48},{72,56},{96,80},{104,88},{128,112},{136,12... | collective-permute-start | bytes 393224 | tf_op jit(solution)/shard_map/ppermute | solution.py:282
  92.7 21.8 %collective-permute-start.10 = (f32[4,64,128]{2,1,0:T(8,128)S(1)}, f32[4,64,128]{2,1,0:T(8,128)S(1)}, u32[]{:S(2)}, u32[]{:S(2)}) collective-permute-start(f32[4,64,128]{2,1,0:T(8,128)S(1)} %get-tuple-element.37), channel_id=1, source_target_pairs={{32,24},{40,16},{64,56},{72,48},{96,88},{104,80},{128,120},{136,11... | collective-permute-start | bytes 393224 | tf_op jit(solution)/shard_map/ppermute | solution.py:282

commit v3 on v2

--- a/solution.py
+++ b/solution.py
@@ -64,8 +64,9 @@
     return a, b, (rest - b.astype(F32)).astype(BF16)
 
 
-def prep_kernel(at, q, k, v, o, g, lse, bq, bk, bv, own, send, kvz):
+def prep_kernel(at, q, k, v, o, g, lse, bq, bk, bv, own, send, kvz, *, ctx_count):
     core = at[0] % 2
+    low_chip = at[0] < ctx_count // 2
     for pack, side in ((own, core), (send, 1 - core)):
         base = pl.multiple_of(side * (Q_OWN * HEAD_SIZE), Q_OWN * HEAD_SIZE)
         kv_base = pl.multiple_of(side * (KV_OWN * HEAD_SIZE), KV_OWN * HEAD_SIZE)
@@ -78,17 +79,16 @@
             deltas.append(
                 jnp.sum(grad.astype(F32) * o[:, cols].astype(F32), axis=1, keepdims=True)
             )
+        to = 0 if pack is own else 1
         for h in range(KV_OWN):
             cols = pl.ds(kv_base + h * HEAD_SIZE, HEAD_SIZE)
             kb = (k[:, cols].astype(F32) + bk[:, cols].astype(F32)).astype(BF16)
             vb = (v[:, cols].astype(F32) + bv[:, cols].astype(F32)).astype(BF16)
             pack[AT_K + h] = kb
             pack[AT_V + h] = vb
-            to = 0 if pack is own else 1
-            for late in range(2):
-                rows = slice(late * HALF, (late + 1) * HALF)
-                kvz[to, late, h] = kb[rows]
-                kvz[to, late, KV_OWN + h] = vb[rows]
+            for i, t in ((h, kb), (KV_OWN + h, vb)):
+                kvz[to, 0, i] = t[:HALF]
+                kvz[to, 1, i] = jnp.where(low_chip, pack[AT_G + i, HALF:], t[HALF:])
         delta = jnp.concatenate(deltas + [jnp.zeros((ROWS, HEAD_SIZE - Q_OWN), F32)], axis=1).T
         heads = pl.ds(pl.multiple_of(side * Q_OWN, Q_OWN), Q_OWN)
         stats = jnp.concatenate(
@@ -100,15 +100,15 @@
         pack[AT_ROW] = stats.astype(BF16)
 
 
+def pack_stats(s):
+    n = Q_OWN
+    lse = (s[:n] + s[n : 2 * n]) + s[2 * n : 3 * n]
+    delta = (s[3 * n : 4 * n] + s[4 * n : 5 * n]) + s[5 * n : 6 * n]
+    return lse * LOG2E, delta
+
+
 def row_stats(own, recv):
-    def one(pack):
-        s = pack[AT_ROW].astype(F32)
-        n = Q_OWN
-        lse = (s[:n] + s[n : 2 * n]) + s[2 * n : 3 * n]
-        delta = (s[3 * n : 4 * n] + s[4 * n : 5 * n]) + s[5 * n : 6 * n]
-        return lse * LOG2E, delta
-
-    (la, da), (lb, db) = one(own), one(recv)
+    (la, da), (lb, db) = (pack_stats(p[AT_ROW].astype(F32)) for p in (own, recv))
     return jnp.concatenate([la, lb], axis=1), jnp.concatenate([da, db], axis=1)
 
 
@@ -134,7 +134,7 @@
     return gq, gk, gv
 
 
-def local_kernel(at, own, recv, gq_out, same, other, kv_sums, *, ctx_count):
+def local_kernel(at, own, recv, gq_out, gkv_out, kv_sums, q_late, *, ctx_count):
     kpos = positions(at[0], 0, ctx_count, False)
     qpos = positions(at[0], 1, ctx_count, False)
     bias = jnp.where(kpos <= qpos, 0.0, LOW)
@@ -152,14 +152,42 @@
             gk = tk if gk is None else gk + tk
             gv = tv if gv is None else gv + tv
         for row, t in ((kv, gk * SCALE), (KV_OWN + kv, gv)):
-            same[row] = t[:ROWS]
-            other[row] = t[ROWS:]
+            gkv_out[row] = t
             kv_sums[row : row + 1, :] = jnp.sum(t, axis=0, keepdims=True)
 
 
+    for h in range(GROUP):
+        q_late[h, :HALF] = own[AT_Q + h, HALF:]
+        q_late[h, HALF:] = recv[AT_Q + h, HALF:]
+    q_late[GROUP, :HALF] = own[AT_ROW, :HALF]
+    q_late[GROUP, HALF:] = recv[AT_ROW, :HALF]
+
+
+def extra_kernel(at, own, recv, far, cross, q_late, out, *, ctx_count):
+    k = jnp.concatenate([own[AT_K], recv[AT_K]], axis=0)
+    v = jnp.concatenate([own[AT_V], recv[AT_V]], axis=0)
+    lse, delta = (
+        jnp.concatenate([a[:, HALF:], b[:, HALF:]], axis=1)
+        for a, b in zip(
+            pack_stats(q_late[GROUP, :HALF].astype(F32)), pack_stats(q_late[GROUP, HALF:].astype(F32))
+        )
+    )
+    gk = gv = None
+    for h in range(GROUP):
+        g = jnp.concatenate([far[0, 1, h], cross[1, h]], axis=0)
+        _, tk, tv = head_terms(q_late[h], g, k, v, 0.0, lse[h : h + 1], delta[h : h + 1])
+        gk = tk if gk is None else gk + tk
+        gv = tv if gv is None else gv + tv
+    high_chip = at[0] >= ctx_count // 2
+    out[0] = jnp.where(high_chip, gk * SCALE, 0.0)
+    out[1] = jnp.where(high_chip, gv, 0.0)
+
+
 def remote_kernel(
-    at, own, recv, far, cross, gq_in, kv_sums, gq_same, gq_other, r1s, r1x, r2s, r2x, sums, *, ctx_count
+    at, own, recv, far, cross, gq_in, kv_sums, gq_same, gq_other, r, sums, *, ctx_count
 ):
+    low_chip = at[0] < ctx_count // 2
+    terms = []
     far_kv = (far.at[0, 0], cross.at[0], far.at[0, 1], cross.at[1])
     totals = []
     far_index = (at[0] + ctx_count // 2) % ctx_count
@@ -183,10 +211,14 @@
             gk = tk if gk is None else gk + tk
             gv = tv if gv is None else gv + tv
         for row, t in ((kv, gk * SCALE), (KV_OWN + kv, gv)):
-            for part, out in enumerate((r1s, r1x, r2s, r2x)):
-                out[row] = t[part * HALF : (part + 1) * HALF]
+            terms.append((row, t))
             total = jnp.sum(t, axis=0, keepdims=True) + kv_sums[row : row + 1, :]
             totals.append((Q_OWN + row, total))
+    terms = [t for _, t in sorted(terms, key=lambda t: t[0])]
+    for i in range(2 * KV_OWN):
+        late = i % 2
+        low = terms[KV_OWN * (i // 2) + 1][late * ROWS : (late + 1) * ROWS]
+        r[i] = jnp.where(low_chip, low, terms[i][:ROWS])
     pad = SUM_ROWS - len(totals)
     totals = [t for _, t in sorted(totals, key=lambda t: t[0])] + [jnp.zeros((pad, HEAD_SIZE), F32)]
     sums[...] = jnp.concatenate(totals, axis=0)
@@ -194,6 +226,26 @@
 
 def cross_kernel(at, far, out):
     out[...] = far[1]
+
+
+def kv_kernel(at, gkv, extra, r, same, other, *, ctx_count):
+    low_chip = at[0] < ctx_count // 2
+    for i in range(2 * KV_OWN):
+        for late in range(2):
+            from_low = r[KV_OWN * (i // KV_OWN) + late] if i % KV_OWN else None
+            from_high = r[i] if late == 0 else None
+            zero = jnp.zeros((ROWS, HEAD_SIZE), F32)
+            got = jnp.where(
+                low_chip,
+                zero if from_high is None else from_high,
+                zero if from_low is None else from_low,
+            )
+            for out, block in ((same, 0), (other, 1)):
+                rows = slice(block * ROWS + late * HALF, block * ROWS + (late + 1) * HALF)
+                t = gkv[i, rows] + got[block * HALF : (block + 1) * HALF]
+                if i % KV_OWN == 0:
+                    t = t + extra[i // KV_OWN, rows]
+                out[i, late * HALF : (late + 1) * HALF] = t.astype(BF16)
 
 
 def join_q_kernel(at, same, other, out):
@@ -204,15 +256,14 @@
             out[:, pl.ds(base + h * HEAD_SIZE, HEAD_SIZE)] = part[h]
 
 
-def join_kv_kernel(at, same, other, r1s, r1x, r2s, r2x, out_k, out_v):
+def join_kv_kernel(at, same, other, out_k, out_v):
     core = at[0] % 2
-    for near, first, second, side in ((same, r1s, r2s, core), (other, r1x, r2x, 1 - core)):
+    for part, side in ((same, core), (other, 1 - core)):
         base = pl.multiple_of(side * (KV_OWN * HEAD_SIZE), KV_OWN * HEAD_SIZE)
         for h in range(KV_OWN):
             cols = pl.ds(base + h * HEAD_SIZE, HEAD_SIZE)
-            for out, i in ((out_k, h), (out_v, KV_OWN + h)):
-                out[:HALF, cols] = (near[i, :HALF] + first[i]).astype(BF16)
-                out[HALF:, cols] = (near[i, HALF:] + second[i]).astype(BF16)
+            out_k[:, cols] = part[h]
+            out_v[:, cols] = part[KV_OWN + h]
 
 
 def pair_sums_kernel(at, mine, theirs, out):
@@ -254,7 +305,7 @@
 
     dp = lax.axis_size("dp")
     own, send, kvz = call(
-        prep_kernel,
+        functools.partial(prep_kernel, ctx_count=n),
         [blocks(PACK), blocks(PACK), shape(2, 2, 2 * KV_OWN, HALF, HEAD_SIZE)],
         9,
         moved=4 << 20,
@@ -265,39 +316,46 @@
     recv = held(swapped(send, "ctx", 1))
     own = held(own)
 
-    gq, kv_same, kv_other, kv_sums = call(
+    gq, gkv, kv_sums, q_late = call(
         functools.partial(local_kernel, ctx_count=n),
-        [blocks(Q_OWN, 2 * ROWS, F32)]
-        + [blocks(2 * KV_OWN, ROWS, F32)] * 2
-        + [shape(2 * KV_OWN, HEAD_SIZE, dtype=F32)],
+        [blocks(Q_OWN, 2 * ROWS, F32), blocks(2 * KV_OWN, 2 * ROWS, F32)]
+        + [shape(2 * KV_OWN, HEAD_SIZE, dtype=F32), blocks(GROUP + 1)],
         2,
         flops=700_000_000,
         moved=3 << 20,
     )(at, own, recv)
-
-    def before(x, bit, senders=range(n)):
+    q_late = held(lax.ppermute(q_late, "ctx", [(i, i + chips) for i in range(chips)]))
+
+    def before(x, bit):
         pairs = []
         for s in range(1, lax.axis_size("section")):
-            pairs += [(s * n + c, (s - 1) * n + (c ^ bit)) for c in senders]
+            pairs += [(s * n + c, (s - 1) * n + (c ^ bit)) for c in range(n)]
         return held(lax.ppermute(x, ("section", "ctx"), pairs))
 
-    kv_same, kv_other = before(kv_same, 0), before(kv_other, 1)
     (cross,) = call(cross_kernel, [shape(2, 2 * KV_OWN, HALF, HEAD_SIZE)], 1)(at, far)
     cross = held(swapped(cross, "ctx", 1))
-    gq_same, gq_other, r1s, r1x, r2s, r2x, sums = call(
+    gq_same, gq_other, r, sums = call(
         functools.partial(remote_kernel, ctx_count=n),
         [blocks(Q_OWN)] * 2
-        + [blocks(2 * KV_OWN, HALF, F32)] * 4
-        + [shape(SUM_ROWS, HEAD_SIZE, dtype=F32)],
+        + [blocks(2 * KV_OWN, ROWS, F32), shape(SUM_ROWS, HEAD_SIZE, dtype=F32)],
         6,
         flops=700_000_000,
         moved=4 << 20,
     )(at, own, recv, far, cross, held(gq), held(kv_sums))
 
-    r2s = before(r2s, chips, range(chips))
-    r2x = before(r2x, chips + 1, range(chips))
-    r1s, r1x = before(r1s, chips), before(r1x, chips + 1)
+    r = held(swapped(r, "ctx", chips))
     gq_same, gq_other = before(gq_same, 0), before(gq_other, 1)
+    (extra,) = call(
+        functools.partial(extra_kernel, ctx_count=n),
+        [blocks(2, 2 * ROWS, F32)],
+        5,
+        flops=150_000_000,
+        moved=1 << 20,
+    )(at, own, recv, far, cross, q_late)
+    kv_same, kv_other = call(
+        functools.partial(kv_kernel, ctx_count=n), [blocks(2 * KV_OWN)] * 2, 3, moved=2 << 20
+    )(at, held(gkv), held(extra), r)
+    kv_same, kv_other = before(kv_same, 0), before(kv_other, 1)
     far_sums = held(swapped(sums, "ctx", chips))
     (copies,) = call(
         pair_sums_kernel, [shape(dp, SUM_ROWS, HEAD_SIZE, dtype=F32)], 2, keep=False
@@ -315,8 +373,8 @@
         keep=False,
     )(at, held(sums), held(swapped(sums, "ctx", 1)))
     recv_k, recv_v = call(
-        join_kv_kernel, [shape(ROWS, KV_HEADS * HEAD_SIZE)] * 2, 6, moved=2 << 20, keep=False
-    )(at, kv_same, kv_other, r1s, r1x, r2s, r2x)
+        join_kv_kernel, [shape(ROWS, KV_HEADS * HEAD_SIZE)] * 2, 2, moved=1 << 19, keep=False
+    )(at, kv_same, kv_other)
     (recv_q,) = call(
         join_q_kernel, [shape(ROWS, Q_HEADS * HEAD_SIZE)], 2, moved=1 << 20, keep=False
     )(at, gq_same, gq_other)

time: 116 us -> 111 us (0.957)
  the two profiles are of different devices: /device:TPU:433 before, /device:TPU:80 now
where the time goes in v3:
time: 111 us; the launch traced here: 110 us
  starting transfers between devices  62.5 us (56%)
  waiting for transfers between devices  20.5 us (18%)
  blocking collectives  15.5 us (14%)
  Pallas kernels  10.7 us (10%)
    ppermute x6, starting transfers between devices, swapped(): return lax.ppermute(value, axis, [(i, i ^ bit) for i in range(size)])  35.3 us
    ppermute x4, starting transfers between devices, before(): return held(lax.ppermute(x, ('section', 'ctx'), pairs))  25.3 us
    all_to_all x1, blocking collectives, body(): copies = held(lax.all_to_all(copies, 'dp', 0, 0, tiled=True))  15.5 us
    ppermute x1, waiting for transfers between devices, body(): lax.ppermute(q_late, 'ctx', [(i, i + chips) for i in range(chips)])  12.3 us
    ppermute x6, waiting for transfers between devices, swapped(): return lax.ppermute(value, axis, [(i, i ^ bit) for i in range(size)])  8.2 us
    pallas_call x1, Pallas kernels, body(): call(functools.partial(remote_kernel, ctx_count=n), [blocks(Q_OWN)] * 2 +...  2.72 us
    pallas_call x1, Pallas kernels, body(): call(functools.partial(local_kernel, ctx_count=n), [blocks(Q_OWN, 2 * ROW...  2.67 us
  transfers between devices with their start and end apart: 11, of which 3 were waited for; matrix products, arithmetic and copies ran while one was open for 0% of the time, Pallas kernels for 5%

profile of v3, /device:TPU:80, one launch (start us, length us, event | category | flops | bytes accessed | tf_op | source)
XLA Modules:
  0.0 110.0 jit_solution(8224958718548886802)
XLA Ops:
  0.6 2.2 %shard_map.136 = (bf16[21,128,128]{2,1,0:T(8,128)(2,1)S(1)}, bf16[21,128,128]{2,1,0:T(8,128)(2,1)S(1)}, bf16[2,2,4,64,128]{4,3,2,1,0:T(8,128)(2,1)S(1)}) custom-call(s32[1]{0:T(128)} %bitcast.at, bf16[128,2048]{1,0:T(8,128)(2,1)} %bitcast.11, bf16[128,512]{1,0:T(8,128)(2,1)} %bitcast.14, bf16[128,512]{1,0:T(8,128)(2,1)} %bitcast.15, ...), custom_call_target="tpu_custom_call" | custom-call | bytes 4194304 | tf_op jit(solution)/shard_map/pallas_call | solution.py:307
  2.8 1.9 %collective-permute-start = (bf16[21,128,128]{2,1,0:T(8,128)(2,1)S(1)}, bf16[21,128,128]{2,1,0:T(8,128)(2,1)S(1)}, u32[]{:S(2)}, u32[]{:S(2)}) collective-permute-start(bf16[21,128,128]{2,1,0:T(8,128)(2,1)S(1)} %get-tuple-element.25), channel_id=1, source_target_pairs={{0,8},{8,0},{16,24},{24,16},{1,9},{9,1},{17,25},{25,17},{2,10},{10... | collective-permute-start | bytes 2064392 | tf_op jit(solution)/shard_map/ppermute | solution.py:297
  4.7 14.6 %collective-permute-start.1 = (bf16[2,2,4,64,128]{4,3,2,1,0:T(8,128)(2,1)S(1)}, bf16[2,2,4,64,128]{4,3,2,1,0:T(8,128)(2,1)S(1)}, u32[]{:S(2)}, u32[]{:S(2)}) collective-permute-start(bf16[2,2,4,64,128]{4,3,2,1,0:T(8,128)(2,1)S(1)} %get-tuple-element.26), channel_id=1, source_target_pairs={{0,16},{8,24},{16,0},{24,8},{1,17},{9,25},{17,1},{25,9},{2,18},{10... | collective-permute-start | bytes 786440 | tf_op jit(solution)/shard_map/ppermute | solution.py:297
  19.3 7.1 %collective-permute-done.1.far = bf16[2,2,4,64,128]{4,3,2,1,0:T(8,128)(2,1)S(1)} collective-permute-done((bf16[2,2,4,64,128]{4,3,2,1,0:T(8,128)(2,1)S(1)}, bf16[2,2,4,64,128]{4,3,2,1,0:T(8,128)(2,1)S(1)}, u32[]{:S(2)}, u32[]{:S(2)}) %collective-permute-start.1) | collective-permute-done | bytes 262176 | tf_op jit(solution)/shard_map/ppermute | solution.py:297
  26.4 1.9 %collective-permute-start.2 = (bf16[2,4,64,128]{3,2,1,0:T(8,128)(2,1)S(1)}, bf16[2,4,64,128]{3,2,1,0:T(8,128)(2,1)S(1)}, u32[]{:S(2)}, u32[]{:S(2)}) collective-permute-start(bf16[2,4,64,128]{3,2,1,0:T(8,128)(2,1)S(1)} %shard_map.137), channel_id=1, source_target_pairs={{0,8},{8,0},{16,24},{24,16},{1,9},{9,1},{17,25},{25,17},{2,10},{10... | collective-permute-start | bytes 393224 | tf_op jit(solution)/shard_map/ppermute | solution.py:297
  28.3 0.0 collective-permute-done.recv
  28.3 2.7 %shard_map.138 = (f32[8,256,128]{2,1,0:T(8,128)S(1)}, f32[4,256,128]{2,1,0:T(8,128)S(1)}, f32[4,128]{1,0:T(4,128)S(1)}, bf16[5,128,128]{2,1,0:T(8,128)(2,1)S(1)}) custom-call(s32[1]{0:T(128)} %bitcast.at, bf16[21,128,128]{2,1,0:T(8,128)(2,1)S(1)} %get-tuple-element.24.own, bf16[21,128,128]{2,1,0:T(8,128)(2,1)S(1)} %collective-permute-done.recv), custom_call_target="tpu_custom_call" | custom-call | flops 700000000 | bytes 3145728 | tf_op jit(solution)/shard_map/pallas_call | solution.py:319
  31.0 0.0 collective-permute-done.2.cross
  31.0 2.7 %shard_map.139 = (bf16[8,128,128]{2,1,0:T(8,128)(2,1)S(1)}, bf16[8,128,128]{2,1,0:T(8,128)(2,1)S(1)}, f32[4,128,128]{2,1,0:T(8,128)S(1)}, f32[16,128]{1,0:T(8,128)S(1)}) custom-call(s32[1]{0:T(128)} %bitcast.at, bf16[21,128,128]{2,1,0:T(8,128)(2,1)S(1)} %get-tuple-element.24.own, bf16[21,128,128]{2,1,0:T(8,128)(2,1)S(1)} %collective-permute-done.recv, ...), custom_call_target="tpu_custom_call" | custom-call | flops 700000000 | bytes 4194304 | tf_op jit(solution)/shard_map/pallas_call | solution.py:337
  33.7 13.1 %collective-permute-start.6 = (f32[4,128,128]{2,1,0:T(8,128)S(1)}, f32[4,128,128]{2,1,0:T(8,128)S(1)}, u32[]{:S(2)}, u32[]{:S(2)}) collective-permute-start(f32[4,128,128]{2,1,0:T(8,128)S(1)} %get-tuple-element.33), channel_id=1, source_target_pairs={{0,16},{8,24},{16,0},{24,8},{1,17},{9,25},{17,1},{25,9},{2,18},{10... | collective-permute-start | bytes 786440 | tf_op jit(solution)/shard_map/ppermute | solution.py:297
  46.8 1.9 %collective-permute-start.5 = (bf16[5,128,128]{2,1,0:T(8,128)(2,1)S(1)}, bf16[5,128,128]{2,1,0:T(8,128)(2,1)S(1)}, u32[]{:S(2)}, u32[]{:S(2)}) collective-permute-start(bf16[5,128,128]{2,1,0:T(8,128)(2,1)S(1)} %get-tuple-element.32), channel_id=1, source_target_pairs={{0,16},{8,24},{1,17},{9,25},{2,18},{10,26},{3,19},{11,27},{4,20},{... | collective-permute-start | bytes 491528 | tf_op jit(solution)/shard_map/ppermute | solution.py:327
  48.8 8.9 %collective-permute-start.3 = (bf16[8,128,128]{2,1,0:T(8,128)(2,1)S(1)}, bf16[8,128,128]{2,1,0:T(8,128)(2,1)S(1)}, u32[]{:S(2)}, u32[]{:S(2)}) collective-permute-start(bf16[8,128,128]{2,1,0:T(8,128)(2,1)S(1)} %get-tuple-element.29), channel_id=1, source_target_pairs={{32,0},{40,8},{48,16},{56,24},{64,32},{72,40},{80,48},{88,56},{96,... | collective-permute-start | bytes 786440 | tf_op jit(solution)/shard_map/ppermute | solution.py:333
  57.7 1.9 %collective-permute-start.4 = (bf16[8,128,128]{2,1,0:T(8,128)(2,1)S(1)}, bf16[8,128,128]{2,1,0:T(8,128)(2,1)S(1)}, u32[]{:S(2)}, u32[]{:S(2)}) collective-permute-start(bf16[8,128,128]{2,1,0:T(8,128)(2,1)S(1)} %get-tuple-element.30), channel_id=1, source_target_pairs={{32,8},{40,0},{48,24},{56,16},{64,40},{72,32},{80,56},{88,48},{96,... | collective-permute-start | bytes 786440 | tf_op jit(solution)/shard_map/ppermute | solution.py:333
  59.6 1.9 %collective-permute-start.9 = (f32[16,128]{1,0:T(8,128)S(1)}, f32[16,128]{1,0:T(8,128)S(1)}, u32[]{:S(2)}, u32[]{:S(2)}) collective-permute-start(f32[16,128]{1,0:T(8,128)S(1)} %get-tuple-element.38.mine), channel_id=1, source_target_pairs={{0,16},{8,24},{16,0},{24,8},{1,17},{9,25},{17,1},{25,9},{2,18},{10... | collective-permute-start | bytes 24584 | tf_op jit(solution)/shard_map/ppermute | solution.py:297
  61.5 12.3 %collective-permute-done.5.q_late = bf16[5,128,128]{2,1,0:T(8,128)(2,1)S(1)} collective-permute-done((bf16[5,128,128]{2,1,0:T(8,128)(2,1)S(1)}, bf16[5,128,128]{2,1,0:T(8,128)(2,1)S(1)}, u32[]{:S(2)}, u32[]{:S(2)}) %collective-permute-start.5) | collective-permute-done | bytes 163872 | tf_op jit(solution)/shard_map/ppermute | solution.py:327
  73.8 0.8 shard_map.141.extra
  74.6 0.0 collective-permute-done.6.r
  74.6 0.1 shard_map.142
  74.7 1.9 %collective-permute-start.7 = (bf16[4,128,128]{2,1,0:T(8,128)(2,1)S(1)}, bf16[4,128,128]{2,1,0:T(8,128)(2,1)S(1)}, u32[]{:S(2)}, u32[]{:S(2)}) collective-permute-start(bf16[4,128,128]{2,1,0:T(8,128)(2,1)S(1)} %get-tuple-element.34), channel_id=1, source_target_pairs={{32,0},{40,8},{48,16},{56,24},{64,32},{72,40},{80,48},{88,56},{96,... | collective-permute-start | bytes 393224 | tf_op jit(solution)/shard_map/ppermute | solution.py:333
  76.6 12.6 %collective-permute-start.8 = (bf16[4,128,128]{2,1,0:T(8,128)(2,1)S(1)}, bf16[4,128,128]{2,1,0:T(8,128)(2,1)S(1)}, u32[]{:S(2)}, u32[]{:S(2)}) collective-permute-start(bf16[4,128,128]{2,1,0:T(8,128)(2,1)S(1)} %get-tuple-element.35), channel_id=1, source_target_pairs={{32,8},{40,0},{48,24},{56,16},{64,40},{72,32},{80,56},{88,48},{96,... | collective-permute-start | bytes 393224 | tf_op jit(solution)/shard_map/ppermute | solution.py:333
  89.1 0.0 collective-permute-done.9.theirs
  89.2 15.5 %all_to_all.5.parts = f32[8,16,128]{2,1,0:T(8,128)S(1)} all-to-all(f32[8,16,128]{2,1,0:T(8,128)S(1)} %shard_map.144), channel_id=1, replica_groups=mesh['section'=32,'ctx'=4,'dp'=8] {'dp'}, dimensions={0} | all-to-all | bytes 131072 | tf_op jit(solution)/shard_map/all_to_all | solution.py:363
  104.6 1.9 %collective-permute-start.10 = (f32[16,128]{1,0:T(8,128)S(1)}, f32[16,128]{1,0:T(8,128)S(1)}, u32[]{:S(2)}, u32[]{:S(2)}) collective-permute-start(f32[16,128]{1,0:T(8,128)S(1)} %shard_map.145.same), channel_id=1, source_target_pairs={{0,8},{8,0},{16,24},{24,16},{1,9},{9,1},{17,25},{25,17},{2,10},{10... | collective-permute-start | bytes 24584 | tf_op jit(solution)/shard_map/ppermute | solution.py:297
  106.6 1.1 %collective-permute-done.10.other = f32[16,128]{1,0:T(8,128)S(1)} collective-permute-done((f32[16,128]{1,0:T(8,128)S(1)}, f32[16,128]{1,0:T(8,128)S(1)}, u32[]{:S(2)}, u32[]{:S(2)}) %collective-permute-start.10) | collective-permute-done | bytes 8224 | tf_op jit(solution)/shard_map/ppermute | solution.py:297
  107.7 0.6 shard_map.146
  108.3 0.0 collective-permute-done.3.same
  108.3 0.0 collective-permute-done.4.other
  108.3 0.9 shard_map.140
  109.3 0.0 collective-permute-done.7.same
  109.3 0.0 collective-permute-done.8.other
  109.3 0.7 shard_map.143
  (3 shorter events, 0.0 us)
Async XLA Ops:
  2.8 25.5 %collective-permute-start = (bf16[21,128,128]{2,1,0:T(8,128)(2,1)S(1)}, bf16[21,128,128]{2,1,0:T(8,128)(2,1)S(1)}, u32[]{:S(2)}, u32[]{:S(2)}) collective-permute-start(bf16[21,128,128]{2,1,0:T(8,128)(2,1)S(1)} %get-tuple-element.25), channel_id=1, source_target_pairs={{0,8},{8,0},{16,24},{24,16},{1,9},{9,1},{17,25},{25,17},{2,10},{10... | collective-permute-start | bytes 2064392 | tf_op jit(solution)/shard_map/ppermute | solution.py:297
  4.7 21.6 %collective-permute-start.1 = (bf16[2,2,4,64,128]{4,3,2,1,0:T(8,128)(2,1)S(1)}, bf16[2,2,4,64,128]{4,3,2,1,0:T(8,128)(2,1)S(1)}, u32[]{:S(2)}, u32[]{:S(2)}) collective-permute-start(bf16[2,2,4,64,128]{4,3,2,1,0:T(8,128)(2,1)S(1)} %get-tuple-element.26), channel_id=1, source_target_pairs={{0,16},{8,24},{16,0},{24,8},{1,17},{9,25},{17,1},{25,9},{2,18},{10... | collective-permute-start | bytes 786440 | tf_op jit(solution)/shard_map/ppermute | solution.py:297
  26.4 4.6 %collective-permute-start.2 = (bf16[2,4,64,128]{3,2,1,0:T(8,128)(2,1)S(1)}, bf16[2,4,64,128]{3,2,1,0:T(8,128)(2,1)S(1)}, u32[]{:S(2)}, u32[]{:S(2)}) collective-permute-start(bf16[2,4,64,128]{3,2,1,0:T(8,128)(2,1)S(1)} %shard_map.137), channel_id=1, source_target_pairs={{0,8},{8,0},{16,24},{24,16},{1,9},{9,1},{17,25},{25,17},{2,10},{10... | collective-permute-start | bytes 393224 | tf_op jit(solution)/shard_map/ppermute | solution.py:297
  33.7 40.9 %collective-permute-start.6 = (f32[4,128,128]{2,1,0:T(8,128)S(1)}, f32[4,128,128]{2,1,0:T(8,128)S(1)}, u32[]{:S(2)}, u32[]{:S(2)}) collective-permute-start(f32[4,128,128]{2,1,0:T(8,128)S(1)} %get-tuple-element.33), channel_id=1, source_target_pairs={{0,16},{8,24},{16,0},{24,8},{1,17},{9,25},{17,1},{25,9},{2,18},{10... | collective-permute-start | bytes 786440 | tf_op jit(solution)/shard_map/ppermute | solution.py:297
  46.8 27.0 %collective-permute-start.5 = (bf16[5,128,128]{2,1,0:T(8,128)(2,1)S(1)}, bf16[5,128,128]{2,1,0:T(8,128)(2,1)S(1)}, u32[]{:S(2)}, u32[]{:S(2)}) collective-permute-start(bf16[5,128,128]{2,1,0:T(8,128)(2,1)S(1)} %get-tuple-element.32), channel_id=1, source_target_pairs={{0,16},{8,24},{1,17},{9,25},{2,18},{10,26},{3,19},{11,27},{4,20},{... | collective-permute-start | bytes 491528 | tf_op jit(solution)/shard_map/ppermute | solution.py:327
  48.8 59.6 %collective-permute-start.3 = (bf16[8,128,128]{2,1,0:T(8,128)(2,1)S(1)}, bf16[8,128,128]{2,1,0:T(8,128)(2,1)S(1)}, u32[]{:S(2)}, u32[]{:S(2)}) collective-permute-start(bf16[8,128,128]{2,1,0:T(8,128)(2,1)S(1)} %get-tuple-element.29), channel_id=1, source_target_pairs={{32,0},{40,8},{48,16},{56,24},{64,32},{72,40},{80,48},{88,56},{96,... | collective-permute-start | bytes 786440 | tf_op jit(solution)/shard_map/ppermute | solution.py:333
  57.7 50.7 %collective-permute-start.4 = (bf16[8,128,128]{2,1,0:T(8,128)(2,1)S(1)}, bf16[8,128,128]{2,1,0:T(8,128)(2,1)S(1)}, u32[]{:S(2)}, u32[]{:S(2)}) collective-permute-start(bf16[8,128,128]{2,1,0:T(8,128)(2,1)S(1)} %get-tuple-element.30), channel_id=1, source_target_pairs={{32,8},{40,0},{48,24},{56,16},{64,40},{72,32},{80,56},{88,48},{96,... | collective-permute-start | bytes 786440 | tf_op jit(solution)/shard_map/ppermute | solution.py:333
  59.6 29.5 %collective-permute-start.9 = (f32[16,128]{1,0:T(8,128)S(1)}, f32[16,128]{1,0:T(8,128)S(1)}, u32[]{:S(2)}, u32[]{:S(2)}) collective-permute-start(f32[16,128]{1,0:T(8,128)S(1)} %get-tuple-element.38.mine), channel_id=1, source_target_pairs={{0,16},{8,24},{16,0},{24,8},{1,17},{9,25},{17,1},{25,9},{2,18},{10... | collective-permute-start | bytes 24584 | tf_op jit(solution)/shard_map/ppermute | solution.py:297
  74.7 34.6 %collective-permute-start.7 = (bf16[4,128,128]{2,1,0:T(8,128)(2,1)S(1)}, bf16[4,128,128]{2,1,0:T(8,128)(2,1)S(1)}, u32[]{:S(2)}, u32[]{:S(2)}) collective-permute-start(bf16[4,128,128]{2,1,0:T(8,128)(2,1)S(1)} %get-tuple-element.34), channel_id=1, source_target_pairs={{32,0},{40,8},{48,16},{56,24},{64,32},{72,40},{80,48},{88,56},{96,... | collective-permute-start | bytes 393224 | tf_op jit(solution)/shard_map/ppermute | solution.py:333
  76.6 32.7 %collective-permute-start.8 = (bf16[4,128,128]{2,1,0:T(8,128)(2,1)S(1)}, bf16[4,128,128]{2,1,0:T(8,128)(2,1)S(1)}, u32[]{:S(2)}, u32[]{:S(2)}) collective-permute-start(bf16[4,128,128]{2,1,0:T(8,128)(2,1)S(1)} %get-tuple-element.35), channel_id=1, source_target_pairs={{32,8},{40,0},{48,24},{56,16},{64,40},{72,32},{80,56},{88,48},{96,... | collective-permute-start | bytes 393224 | tf_op jit(solution)/shard_map/ppermute | solution.py:333
  104.6 3.1 %collective-permute-start.10 = (f32[16,128]{1,0:T(8,128)S(1)}, f32[16,128]{1,0:T(8,128)S(1)}, u32[]{:S(2)}, u32[]{:S(2)}) collective-permute-start(f32[16,128]{1,0:T(8,128)S(1)} %shard_map.145.same), channel_id=1, source_target_pairs={{0,8},{8,0},{16,24},{24,16},{1,9},{9,1},{17,25},{25,17},{2,10},{10... | collective-permute-start | bytes 24584 | tf_op jit(solution)/shard_map/ppermute | solution.py:297

commit v4 on v3

--- a/solution.py
+++ b/solution.py
@@ -218,22 +218,29 @@
     for i in range(2 * KV_OWN):
         late = i % 2
         low = terms[KV_OWN * (i // 2) + 1][late * ROWS : (late + 1) * ROWS]
-        r[i] = jnp.where(low_chip, low, terms[i][:ROWS])
+        r[i * ROWS : (i + 1) * ROWS, :] = jnp.where(low_chip, low, terms[i][:ROWS])
     pad = SUM_ROWS - len(totals)
     totals = [t for _, t in sorted(totals, key=lambda t: t[0])] + [jnp.zeros((pad, HEAD_SIZE), F32)]
-    sums[...] = jnp.concatenate(totals, axis=0)
+    totals = jnp.concatenate(totals, axis=0)
+    sums[...] = totals
+    r[2 * KV_OWN * ROWS :, :] = totals
 
 
 def cross_kernel(at, far, out):
     out[...] = far[1]
 
 
-def kv_kernel(at, gkv, extra, r, same, other, *, ctx_count):
+def kv_kernel(at, gkv, extra, r, gq_same, gq_other, sums, same, other, copies, *, ctx_count):
     low_chip = at[0] < ctx_count // 2
+    both = sums[...] + r[2 * KV_OWN * ROWS :, :]
+    copies[...] = jnp.broadcast_to(both[None], copies.shape)
+    same[:Q_OWN] = gq_same[...]
+    other[:Q_OWN] = gq_other[...]
+    block_of = lambda i: r[i * ROWS : (i + 1) * ROWS, :]
     for i in range(2 * KV_OWN):
         for late in range(2):
-            from_low = r[KV_OWN * (i // KV_OWN) + late] if i % KV_OWN else None
-            from_high = r[i] if late == 0 else None
+            from_low = block_of(KV_OWN * (i // KV_OWN) + late) if i % KV_OWN else None
+            from_high = block_of(i) if late == 0 else None
             zero = jnp.zeros((ROWS, HEAD_SIZE), F32)
             got = jnp.where(
                 low_chip,
@@ -245,29 +252,20 @@
                 t = gkv[i, rows] + got[block * HALF : (block + 1) * HALF]
                 if i % KV_OWN == 0:
                     t = t + extra[i // KV_OWN, rows]
-                out[i, late * HALF : (late + 1) * HALF] = t.astype(BF16)
-
-
-def join_q_kernel(at, same, other, out):
+                out[Q_OWN + i, late * HALF : (late + 1) * HALF] = t.astype(BF16)
+
+
+def join_kernel(at, same, other, out_q, out_k, out_v):
     core = at[0] % 2
     for part, side in ((same, core), (other, 1 - core)):
         base = pl.multiple_of(side * (Q_OWN * HEAD_SIZE), Q_OWN * HEAD_SIZE)
         for h in range(Q_OWN):
-            out[:, pl.ds(base + h * HEAD_SIZE, HEAD_SIZE)] = part[h]
-
-
-def join_kv_kernel(at, same, other, out_k, out_v):
-    core = at[0] % 2
-    for part, side in ((same, core), (other, 1 - core)):
+            out_q[:, pl.ds(base + h * HEAD_SIZE, HEAD_SIZE)] = part[h]
         base = pl.multiple_of(side * (KV_OWN * HEAD_SIZE), KV_OWN * HEAD_SIZE)
         for h in range(KV_OWN):
             cols = pl.ds(base + h * HEAD_SIZE, HEAD_SIZE)
-            out_k[:, cols] = part[h]
-            out_v[:, cols] = part[KV_OWN + h]
-
-
-def pair_sums_kernel(at, mine, theirs, out):
-    out[...] = jnp.broadcast_to((mine[...] + theirs[...])[None], out.shape)
+            out_k[:, cols] = part[Q_OWN + h]
+            out_v[:, cols] = part[Q_OWN + KV_OWN + h]
 
 
 def replica_sums_kernel(at, parts, out):
@@ -337,14 +335,16 @@
     gq_same, gq_other, r, sums = call(
         functools.partial(remote_kernel, ctx_count=n),
         [blocks(Q_OWN)] * 2
-        + [blocks(2 * KV_OWN, ROWS, F32), shape(SUM_ROWS, HEAD_SIZE, dtype=F32)],
+        + [
+            shape(2 * KV_OWN * ROWS + SUM_ROWS, HEAD_SIZE, dtype=F32),
+            shape(SUM_ROWS, HEAD_SIZE, dtype=F32),
+        ],
         6,
         flops=700_000_000,
         moved=4 << 20,
     )(at, own, recv, far, cross, held(gq), held(kv_sums))
 
     r = held(swapped(r, "ctx", chips))
-    gq_same, gq_other = before(gq_same, 0), before(gq_other, 1)
     (extra,) = call(
         functools.partial(extra_kernel, ctx_count=n),
         [blocks(2, 2 * ROWS, F32)],
@@ -352,14 +352,14 @@
         flops=150_000_000,
         moved=1 << 20,
     )(at, own, recv, far, cross, q_late)
-    kv_same, kv_other = call(
-        functools.partial(kv_kernel, ctx_count=n), [blocks(2 * KV_OWN)] * 2, 3, moved=2 << 20
-    )(at, held(gkv), held(extra), r)
-    kv_same, kv_other = before(kv_same, 0), before(kv_other, 1)
-    far_sums = held(swapped(sums, "ctx", chips))
-    (copies,) = call(
-        pair_sums_kernel, [shape(dp, SUM_ROWS, HEAD_SIZE, dtype=F32)], 2, keep=False
-    )(at, held(sums), far_sums)
+    same, other, copies = call(
+        functools.partial(kv_kernel, ctx_count=n),
+        [blocks(Q_OWN + 2 * KV_OWN)] * 2 + [shape(dp, SUM_ROWS, HEAD_SIZE, dtype=F32)],
+        6,
+        moved=2 << 20,
+        keep=2,
+    )(at, held(gkv), held(extra), r, held(gq_same), held(gq_other), held(sums))
+    same, other = before(same, 0), before(other, 1)
     copies = held(lax.all_to_all(copies, "dp", 0, 0, tiled=True))
     (sums,) = call(replica_sums_kernel, [shape(SUM_ROWS, HEAD_SIZE, dtype=F32)], 1)(at, copies)
     sum_q, sum_k, sum_v = call(
@@ -372,12 +372,13 @@
         2,
         keep=False,
     )(at, held(sums), held(swapped(sums, "ctx", 1)))
-    recv_k, recv_v = call(
-        join_kv_kernel, [shape(ROWS, KV_HEADS * HEAD_SIZE)] * 2, 2, moved=1 << 19, keep=False
-    )(at, kv_same, kv_other)
-    (recv_q,) = call(
-        join_q_kernel, [shape(ROWS, Q_HEADS * HEAD_SIZE)], 2, moved=1 << 20, keep=False
-    )(at, gq_same, gq_other)
+    recv_q, recv_k, recv_v = call(
+        join_kernel,
+        [shape(ROWS, Q_HEADS * HEAD_SIZE)] + [shape(ROWS, KV_HEADS * HEAD_SIZE)] * 2,
+        2,
+        moved=3 << 19,
+        keep=False,
+    )(at, same, other)
     return (recv_q[None, None], recv_k[None, None], recv_v[None, None], sum_q, sum_k, sum_v)
 
 

time: 111 us -> 95.1 us (0.86)
  starting transfers between devices: 62.5 us -> 46.2 us
  waiting for transfers between devices: 20.5 us -> 21.9 us
    ppermute x4 -> x2, starting transfers between devices: 25.3 us -> 10.9 us  [before(): return held(lax.ppermute(x, ('section', 'ctx'), pairs))]
    ppermute x6 -> x5, starting transfers between devices: 35.3 us -> 33.4 us  [swapped(): return lax.ppermute(value, axis, [(i, i ^ bit) for i in range(size)])]
    ppermute x1, waiting for transfers between devices: 12.3 us -> 13.7 us  [body(): lax.ppermute(q_late, 'ctx', [(i, i + chips) for i in range(chips)])]
    ppermute x6 -> x5, waiting for transfers between devices: 8.2 us -> 8.2 us  [swapped(): return lax.ppermute(value, axis, [(i, i ^ bit) for i in range(size)])]
  transfers between devices with their start and end apart: 11 -> 8, of which waited for: 3 -> 3; matrix products, arithmetic and copies ran while one was open for 0% -> 0% of each run, Pallas kernels for 5% -> 4%
where the time goes in v4:
time: 95.1 us; the launch traced here: 94.4 us
  starting transfers between devices  46.2 us (49%)
  waiting for transfers between devices  21.9 us (23%)
  blocking collectives  15.3 us (16%)
  Pallas kernels  10.2 us (11%)
    ppermute x5, starting transfers between devices, swapped(): return lax.ppermute(value, axis, [(i, i ^ bit) for i in range(size)])  33.4 us
    all_to_all x1, blocking collectives, body(): copies = held(lax.all_to_all(copies, 'dp', 0, 0, tiled=True))  15.3 us
    ppermute x1, waiting for transfers between devices, body(): lax.ppermute(q_late, 'ctx', [(i, i + chips) for i in range(chips)])  13.7 us
    ppermute x2, starting transfers between devices, before(): return held(lax.ppermute(x, ('section', 'ctx'), pairs))  10.9 us
    ppermute x5, waiting for transfers between devices, swapped(): return lax.ppermute(value, axis, [(i, i ^ bit) for i in range(size)])  8.2 us
    pallas_call x1, Pallas kernels, body(): call(functools.partial(remote_kernel, ctx_count=n), [blocks(Q_OWN)] * 2 +...  2.73 us
    pallas_call x1, Pallas kernels, body(): call(functools.partial(local_kernel, ctx_count=n), [blocks(Q_OWN, 2 * ROW...  2.69 us
    pallas_call x1, Pallas kernels, body(): call(functools.partial(prep_kernel, ctx_count=n), [blocks(PACK), blocks(P...  2.18 us
  transfers between devices with their start and end apart: 8, of which 3 were waited for; matrix products, arithmetic and copies ran while one was open for 0% of the time, Pallas kernels for 4%

profile of v4, /device:TPU:80, one launch (start us, length us, event | category | flops | bytes accessed | tf_op | source)
XLA Modules:
  0.0 94.4 jit_solution(18407244809950944629)
XLA Ops:
  0.6 2.2 %shard_map.136 = (bf16[21,128,128]{2,1,0:T(8,128)(2,1)S(1)}, bf16[21,128,128]{2,1,0:T(8,128)(2,1)S(1)}, bf16[2,2,4,64,128]{4,3,2,1,0:T(8,128)(2,1)S(1)}) custom-call(s32[1]{0:T(128)} %bitcast.at, bf16[128,2048]{1,0:T(8,128)(2,1)} %bitcast.10, bf16[128,512]{1,0:T(8,128)(2,1)} %bitcast.13, bf16[128,512]{1,0:T(8,128)(2,1)} %bitcast.14, ...), custom_call_target="tpu_custom_call" | custom-call | bytes 4194304 | tf_op jit(solution)/shard_map/pallas_call | solution.py:305
  2.8 1.9 %collective-permute-start = (bf16[21,128,128]{2,1,0:T(8,128)(2,1)S(1)}, bf16[21,128,128]{2,1,0:T(8,128)(2,1)S(1)}, u32[]{:S(2)}, u32[]{:S(2)}) collective-permute-start(bf16[21,128,128]{2,1,0:T(8,128)(2,1)S(1)} %get-tuple-element.27), channel_id=1, source_target_pairs={{0,8},{8,0},{16,24},{24,16},{1,9},{9,1},{17,25},{25,17},{2,10},{10... | collective-permute-start | bytes 2064392 | tf_op jit(solution)/shard_map/ppermute | solution.py:295
  4.7 14.6 %collective-permute-start.1 = (bf16[2,2,4,64,128]{4,3,2,1,0:T(8,128)(2,1)S(1)}, bf16[2,2,4,64,128]{4,3,2,1,0:T(8,128)(2,1)S(1)}, u32[]{:S(2)}, u32[]{:S(2)}) collective-permute-start(bf16[2,2,4,64,128]{4,3,2,1,0:T(8,128)(2,1)S(1)} %get-tuple-element.29), channel_id=1, source_target_pairs={{0,16},{8,24},{16,0},{24,8},{1,17},{9,25},{17,1},{25,9},{2,18},{10... | collective-permute-start | bytes 786440 | tf_op jit(solution)/shard_map/ppermute | solution.py:295
  19.3 7.1 %collective-permute-done.1.far = bf16[2,2,4,64,128]{4,3,2,1,0:T(8,128)(2,1)S(1)} collective-permute-done((bf16[2,2,4,64,128]{4,3,2,1,0:T(8,128)(2,1)S(1)}, bf16[2,2,4,64,128]{4,3,2,1,0:T(8,128)(2,1)S(1)}, u32[]{:S(2)}, u32[]{:S(2)}) %collective-permute-start.1) | collective-permute-done | bytes 262176 | tf_op jit(solution)/shard_map/ppermute | solution.py:295
  26.4 1.9 %collective-permute-start.2 = (bf16[2,4,64,128]{3,2,1,0:T(8,128)(2,1)S(1)}, bf16[2,4,64,128]{3,2,1,0:T(8,128)(2,1)S(1)}, u32[]{:S(2)}, u32[]{:S(2)}) collective-permute-start(bf16[2,4,64,128]{3,2,1,0:T(8,128)(2,1)S(1)} %shard_map.138), channel_id=1, source_target_pairs={{0,8},{8,0},{16,24},{24,16},{1,9},{9,1},{17,25},{25,17},{2,10},{10... | collective-permute-start | bytes 393224 | tf_op jit(solution)/shard_map/ppermute | solution.py:295
  28.3 0.0 collective-permute-done.recv
  28.3 2.7 %shard_map.137 = (f32[8,256,128]{2,1,0:T(8,128)S(1)}, f32[4,256,128]{2,1,0:T(8,128)S(1)}, f32[4,128]{1,0:T(4,128)S(1)}, bf16[5,128,128]{2,1,0:T(8,128)(2,1)S(1)}) custom-call(s32[1]{0:T(128)} %bitcast.at, bf16[21,128,128]{2,1,0:T(8,128)(2,1)S(1)} %get-tuple-element.26.own, bf16[21,128,128]{2,1,0:T(8,128)(2,1)S(1)} %collective-permute-done.recv), custom_call_target="tpu_custom_call" | custom-call | flops 700000000 | bytes 3145728 | tf_op jit(solution)/shard_map/pallas_call | solution.py:317
  31.0 0.0 collective-permute-done.2.cross
  31.0 2.7 %shard_map.140 = (bf16[8,128,128]{2,1,0:T(8,128)(2,1)S(1)}, bf16[8,128,128]{2,1,0:T(8,128)(2,1)S(1)}, f32[528,128]{1,0:T(8,128)S(1)}, f32[16,128]{1,0:T(8,128)S(1)}) custom-call(s32[1]{0:T(128)} %bitcast.at, bf16[21,128,128]{2,1,0:T(8,128)(2,1)S(1)} %get-tuple-element.26.own, bf16[21,128,128]{2,1,0:T(8,128)(2,1)S(1)} %collective-permute-done.recv, ...), custom_call_target="tpu_custom_call" | custom-call | flops 700000000 | bytes 4194304 | tf_op jit(solution)/shard_map/pallas_call | solution.py:335
  33.8 13.1 %collective-permute-start.4 = (f32[528,128]{1,0:T(8,128)S(1)}, f32[528,128]{1,0:T(8,128)S(1)}, u32[]{:S(2)}, u32[]{:S(2)}) collective-permute-start(f32[528,128]{1,0:T(8,128)S(1)} %get-tuple-element.33), channel_id=1, source_target_pairs={{0,16},{8,24},{16,0},{24,8},{1,17},{9,25},{17,1},{25,9},{2,18},{10... | collective-permute-start | bytes 811016 | tf_op jit(solution)/shard_map/ppermute | solution.py:295
  46.9 1.9 %collective-permute-start.3 = (bf16[5,128,128]{2,1,0:T(8,128)(2,1)S(1)}, bf16[5,128,128]{2,1,0:T(8,128)(2,1)S(1)}, u32[]{:S(2)}, u32[]{:S(2)}) collective-permute-start(bf16[5,128,128]{2,1,0:T(8,128)(2,1)S(1)} %get-tuple-element.30), channel_id=1, source_target_pairs={{0,16},{8,24},{1,17},{9,25},{2,18},{10,26},{3,19},{11,27},{4,20},{... | collective-permute-start | bytes 491528 | tf_op jit(solution)/shard_map/ppermute | solution.py:325
  48.8 13.7 %collective-permute-done.3.q_late = bf16[5,128,128]{2,1,0:T(8,128)(2,1)S(1)} collective-permute-done((bf16[5,128,128]{2,1,0:T(8,128)(2,1)S(1)}, bf16[5,128,128]{2,1,0:T(8,128)(2,1)S(1)}, u32[]{:S(2)}, u32[]{:S(2)}) %collective-permute-start.3) | collective-permute-done | bytes 163872 | tf_op jit(solution)/shard_map/ppermute | solution.py:325
  62.5 0.8 shard_map.139.extra
  63.3 0.0 collective-permute-done.4.r
  63.3 0.1 shard_map.141
  63.4 2.4 %collective-permute-start.5 = (bf16[12,128,128]{2,1,0:T(8,128)(2,1)S(1)}, bf16[12,128,128]{2,1,0:T(8,128)(2,1)S(1)}, u32[]{:S(2)}, u32[]{:S(2)}) collective-permute-start(bf16[12,128,128]{2,1,0:T(8,128)(2,1)S(1)} %get-tuple-element.37), channel_id=1, source_target_pairs={{32,0},{40,8},{48,16},{56,24},{64,32},{72,40},{80,48},{88,56},{96,... | collective-permute-start | bytes 1179656 | tf_op jit(solution)/shard_map/ppermute | solution.py:331
  65.8 8.5 %collective-permute-start.6 = (bf16[12,128,128]{2,1,0:T(8,128)(2,1)S(1)}, bf16[12,128,128]{2,1,0:T(8,128)(2,1)S(1)}, u32[]{:S(2)}, u32[]{:S(2)}) collective-permute-start(bf16[12,128,128]{2,1,0:T(8,128)(2,1)S(1)} %get-tuple-element.38), channel_id=1, source_target_pairs={{32,8},{40,0},{48,24},{56,16},{64,40},{72,32},{80,56},{88,48},{96,... | collective-permute-start | bytes 1179656 | tf_op jit(solution)/shard_map/ppermute | solution.py:331
  74.3 15.3 %all_to_all.5.parts = f32[8,16,128]{2,1,0:T(8,128)S(1)} all-to-all(f32[8,16,128]{2,1,0:T(8,128)S(1)} %get-tuple-element.42), channel_id=1, replica_groups=mesh['section'=32,'ctx'=4,'dp'=8] {'dp'}, dimensions={0} | all-to-all | bytes 131072 | tf_op jit(solution)/shard_map/all_to_all | solution.py:363
  89.6 1.9 %collective-permute-start.7 = (f32[16,128]{1,0:T(8,128)S(1)}, f32[16,128]{1,0:T(8,128)S(1)}, u32[]{:S(2)}, u32[]{:S(2)}) collective-permute-start(f32[16,128]{1,0:T(8,128)S(1)} %shard_map.143.same), channel_id=1, source_target_pairs={{0,8},{8,0},{16,24},{24,16},{1,9},{9,1},{17,25},{25,17},{2,10},{10... | collective-permute-start | bytes 24584 | tf_op jit(solution)/shard_map/ppermute | solution.py:295
  91.6 1.1 %collective-permute-done.7.other = f32[16,128]{1,0:T(8,128)S(1)} collective-permute-done((f32[16,128]{1,0:T(8,128)S(1)}, f32[16,128]{1,0:T(8,128)S(1)}, u32[]{:S(2)}, u32[]{:S(2)}) %collective-permute-start.7) | collective-permute-done | bytes 8224 | tf_op jit(solution)/shard_map/ppermute | solution.py:295
  92.7 0.6 shard_map.144
  93.3 0.0 collective-permute-done.5.same
  93.3 0.0 collective-permute-done.6.other
  93.3 1.0 %shard_map.142 = (bf16[128,2048]{1,0:T(8,128)(2,1)}, bf16[128,512]{1,0:T(8,128)(2,1)}, bf16[128,512]{1,0:T(8,128)(2,1)}) custom-call(s32[1]{0:T(128)} %bitcast.at, bf16[12,128,128]{2,1,0:T(8,128)(2,1)S(1)} %collective-permute-done.5.same, bf16[12,128,128]{2,1,0:T(8,128)(2,1)S(1)} %collective-permute-done.6.other), custom_call_target="tpu_custom_call" | custom-call | bytes 1572864 | tf_op jit(solution)/shard_map/pallas_call | solution.py:375
  (2 shorter events, 0.0 us)
Async XLA Ops:
  2.8 25.5 %collective-permute-start = (bf16[21,128,128]{2,1,0:T(8,128)(2,1)S(1)}, bf16[21,128,128]{2,1,0:T(8,128)(2,1)S(1)}, u32[]{:S(2)}, u32[]{:S(2)}) collective-permute-start(bf16[21,128,128]{2,1,0:T(8,128)(2,1)S(1)} %get-tuple-element.27), channel_id=1, source_target_pairs={{0,8},{8,0},{16,24},{24,16},{1,9},{9,1},{17,25},{25,17},{2,10},{10... | collective-permute-start | bytes 2064392 | tf_op jit(solution)/shard_map/ppermute | solution.py:295
  4.7 21.6 %collective-permute-start.1 = (bf16[2,2,4,64,128]{4,3,2,1,0:T(8,128)(2,1)S(1)}, bf16[2,2,4,64,128]{4,3,2,1,0:T(8,128)(2,1)S(1)}, u32[]{:S(2)}, u32[]{:S(2)}) collective-permute-start(bf16[2,2,4,64,128]{4,3,2,1,0:T(8,128)(2,1)S(1)} %get-tuple-element.29), channel_id=1, source_target_pairs={{0,16},{8,24},{16,0},{24,8},{1,17},{9,25},{17,1},{25,9},{2,18},{10... | collective-permute-start | bytes 786440 | tf_op jit(solution)/shard_map/ppermute | solution.py:295
  26.4 4.6 %collective-permute-start.2 = (bf16[2,4,64,128]{3,2,1,0:T(8,128)(2,1)S(1)}, bf16[2,4,64,128]{3,2,1,0:T(8,128)(2,1)S(1)}, u32[]{:S(2)}, u32[]{:S(2)}) collective-permute-start(bf16[2,4,64,128]{3,2,1,0:T(8,128)(2,1)S(1)} %shard_map.138), channel_id=1, source_target_pairs={{0,8},{8,0},{16,24},{24,16},{1,9},{9,1},{17,25},{25,17},{2,10},{10... | collective-permute-start | bytes 393224 | tf_op jit(solution)/shard_map/ppermute | solution.py:295
  33.8 29.5 %collective-permute-start.4 = (f32[528,128]{1,0:T(8,128)S(1)}, f32[528,128]{1,0:T(8,128)S(1)}, u32[]{:S(2)}, u32[]{:S(2)}) collective-permute-start(f32[528,128]{1,0:T(8,128)S(1)} %get-tuple-element.33), channel_id=1, source_target_pairs={{0,16},{8,24},{16,0},{24,8},{1,17},{9,25},{17,1},{25,9},{2,18},{10... | collective-permute-start | bytes 811016 | tf_op jit(solution)/shard_map/ppermute | solution.py:295
  46.9 15.7 %collective-permute-start.3 = (bf16[5,128,128]{2,1,0:T(8,128)(2,1)S(1)}, bf16[5,128,128]{2,1,0:T(8,128)(2,1)S(1)}, u32[]{:S(2)}, u32[]{:S(2)}) collective-permute-start(bf16[5,128,128]{2,1,0:T(8,128)(2,1)S(1)} %get-tuple-element.30), channel_id=1, source_target_pairs={{0,16},{8,24},{1,17},{9,25},{2,18},{10,26},{3,19},{11,27},{4,20},{... | collective-permute-start | bytes 491528 | tf_op jit(solution)/shard_map/ppermute | solution.py:325
  63.4 29.9 %collective-permute-start.5 = (bf16[12,128,128]{2,1,0:T(8,128)(2,1)S(1)}, bf16[12,128,128]{2,1,0:T(8,128)(2,1)S(1)}, u32[]{:S(2)}, u32[]{:S(2)}) collective-permute-start(bf16[12,128,128]{2,1,0:T(8,128)(2,1)S(1)} %get-tuple-element.37), channel_id=1, source_target_pairs={{32,0},{40,8},{48,16},{56,24},{64,32},{72,40},{80,48},{88,56},{96,... | collective-permute-start | bytes 1179656 | tf_op jit(solution)/shard_map/ppermute | solution.py:331
  65.8 27.5 %collective-permute-start.6 = (bf16[12,128,128]{2,1,0:T(8,128)(2,1)S(1)}, bf16[12,128,128]{2,1,0:T(8,128)(2,1)S(1)}, u32[]{:S(2)}, u32[]{:S(2)}) collective-permute-start(bf16[12,128,128]{2,1,0:T(8,128)(2,1)S(1)} %get-tuple-element.38), channel_id=1, source_target_pairs={{32,8},{40,0},{48,24},{56,16},{64,40},{72,32},{80,56},{88,48},{96,... | collective-permute-start | bytes 1179656 | tf_op jit(solution)/shard_map/ppermute | solution.py:331
  89.6 3.1 %collective-permute-start.7 = (f32[16,128]{1,0:T(8,128)S(1)}, f32[16,128]{1,0:T(8,128)S(1)}, u32[]{:S(2)}, u32[]{:S(2)}) collective-permute-start(f32[16,128]{1,0:T(8,128)S(1)} %shard_map.143.same), channel_id=1, source_target_pairs={{0,8},{8,0},{16,24},{24,16},{1,9},{9,1},{17,25},{25,17},{2,10},{10... | collective-permute-start | bytes 24584 | tf_op jit(solution)/shard_map/ppermute | solution.py:295

commit v5 on v4

--- a/solution.py
+++ b/solution.py
@@ -221,19 +221,15 @@
         r[i * ROWS : (i + 1) * ROWS, :] = jnp.where(low_chip, low, terms[i][:ROWS])
     pad = SUM_ROWS - len(totals)
     totals = [t for _, t in sorted(totals, key=lambda t: t[0])] + [jnp.zeros((pad, HEAD_SIZE), F32)]
-    totals = jnp.concatenate(totals, axis=0)
-    sums[...] = totals
-    r[2 * KV_OWN * ROWS :, :] = totals
+    sums[...] = jnp.broadcast_to(jnp.concatenate(totals, axis=0)[None], sums.shape)
 
 
 def cross_kernel(at, far, out):
     out[...] = far[1]
 
 
-def kv_kernel(at, gkv, extra, r, gq_same, gq_other, sums, same, other, copies, *, ctx_count):
+def kv_kernel(at, gkv, extra, r, gq_same, gq_other, same, other, *, ctx_count):
     low_chip = at[0] < ctx_count // 2
-    both = sums[...] + r[2 * KV_OWN * ROWS :, :]
-    copies[...] = jnp.broadcast_to(both[None], copies.shape)
     same[:Q_OWN] = gq_same[...]
     other[:Q_OWN] = gq_other[...]
     block_of = lambda i: r[i * ROWS : (i + 1) * ROWS, :]
@@ -275,9 +271,15 @@
     out[...] = total
 
 
-def join_sums_kernel(at, same, other, out_q, out_k, out_v):
+def stack_kernel(at, same, other, out):
+    out[0] = same[...]
+    out[1] = other[...]
+
+
+def join_sums_kernel(at, chip, far, out_q, out_k, out_v):
     core = at[0] % 2
-    for part, side in ((same, core), (other, 1 - core)):
+    for i, side in ((0, core), (1, 1 - core)):
+        part = chip[i] + far[i]
         base = pl.multiple_of(side * (Q_OWN * HEAD_SIZE), Q_OWN * HEAD_SIZE)
         kv_base = pl.multiple_of(side * (KV_OWN * HEAD_SIZE), KV_OWN * HEAD_SIZE)
         for h in range(Q_OWN):
@@ -336,13 +338,15 @@
         functools.partial(remote_kernel, ctx_count=n),
         [blocks(Q_OWN)] * 2
         + [
-            shape(2 * KV_OWN * ROWS + SUM_ROWS, HEAD_SIZE, dtype=F32),
-            shape(SUM_ROWS, HEAD_SIZE, dtype=F32),
+            shape(2 * KV_OWN * ROWS, HEAD_SIZE, dtype=F32),
+            shape(dp, SUM_ROWS, HEAD_SIZE, dtype=F32),
         ],
         6,
         flops=700_000_000,
         moved=4 << 20,
+        keep=3,
     )(at, own, recv, far, cross, held(gq), held(kv_sums))
+    parts = held(lax.all_to_all(sums, "dp", 0, 0, tiled=True))
 
     r = held(swapped(r, "ctx", chips))
     (extra,) = call(
@@ -352,16 +356,19 @@
         flops=150_000_000,
         moved=1 << 20,
     )(at, own, recv, far, cross, q_late)
-    same, other, copies = call(
+    same, other = call(
         functools.partial(kv_kernel, ctx_count=n),
-        [blocks(Q_OWN + 2 * KV_OWN)] * 2 + [shape(dp, SUM_ROWS, HEAD_SIZE, dtype=F32)],
-        6,
+        [blocks(Q_OWN + 2 * KV_OWN)] * 2,
+        5,
         moved=2 << 20,
-        keep=2,
-    )(at, held(gkv), held(extra), r, held(gq_same), held(gq_other), held(sums))
+    )(at, held(gkv), held(extra), r, held(gq_same), held(gq_other))
     same, other = before(same, 0), before(other, 1)
-    copies = held(lax.all_to_all(copies, "dp", 0, 0, tiled=True))
-    (sums,) = call(replica_sums_kernel, [shape(SUM_ROWS, HEAD_SIZE, dtype=F32)], 1)(at, copies)
+    (sums,) = call(replica_sums_kernel, [shape(SUM_ROWS, HEAD_SIZE, dtype=F32)], 1)(at, parts)
+    sums_other = swapped(sums, "ctx", 1)
+    (chip_sums,) = call(
+        stack_kernel, [shape(2, SUM_ROWS, HEAD_SIZE, dtype=F32)], 2
+    )(at, held(sums), held(sums_other))
+    far_sums = swapped(chip_sums, "ctx", chips)
     sum_q, sum_k, sum_v = call(
         join_sums_kernel,
         [
@@ -371,7 +378,7 @@
         ],
         2,
         keep=False,
-    )(at, held(sums), held(swapped(sums, "ctx", 1)))
+    )(at, held(chip_sums), held(far_sums))
     recv_q, recv_k, recv_v = call(
         join_kernel,
         [shape(ROWS, Q_HEADS * HEAD_SIZE)] + [shape(ROWS, KV_HEADS * HEAD_SIZE)] * 2,

time: 95.1 us -> 104 us (1.094)
  the two profiles are of different devices: /device:TPU:80 before, /device:TPU:96 now
where the time goes in v5:
time: 104 us
  starting transfers between devices  54.5 us (52%)
  waiting for transfers between devices  23.3 us (22%)
  blocking collectives  15.3 us (15%)
  Pallas kernels  10.2 us (10%)
    ppermute x6, starting transfers between devices, swapped(): return lax.ppermute(value, axis, [(i, i ^ bit) for i in range(size)])  41.7 us
    all_to_all x1, blocking collectives, body(): parts = held(lax.all_to_all(sums, 'dp', 0, 0, tiled=True))  15.3 us
    ppermute x1, waiting for transfers between devices, body(): lax.ppermute(q_late, 'ctx', [(i, i + chips) for i in range(chips)])  13.4 us
    ppermute x2, starting transfers between devices, before(): return held(lax.ppermute(x, ('section', 'ctx'), pairs))  10.9 us
    ppermute x6, waiting for transfers between devices, swapped(): return lax.ppermute(value, axis, [(i, i ^ bit) for i in range(size)])  9.9 us
    pallas_call x1, Pallas kernels, body(): call(functools.partial(remote_kernel, ctx_count=n), [blocks(Q_OWN)] * 2 +...  2.73 us
    pallas_call x1, Pallas kernels, body(): call(functools.partial(local_kernel, ctx_count=n), [blocks(Q_OWN, 2 * ROW...  2.7 us
    pallas_call x1, Pallas kernels, body(): call(functools.partial(prep_kernel, ctx_count=n), [blocks(PACK), blocks(P...  2.18 us
  transfers between devices with their start and end apart: 9, of which 4 were waited for; matrix products, arithmetic and copies ran while one was open for 0% of the time, Pallas kernels for 4%

profile of v5, /device:TPU:96, one launch (start us, length us, event | category | flops | bytes accessed | tf_op | source)
XLA Modules:
  0.0 104.0 jit_solution(676384836280175977)
XLA Ops:
  0.6 2.2 %shard_map.136 = (bf16[21,128,128]{2,1,0:T(8,128)(2,1)S(1)}, bf16[21,128,128]{2,1,0:T(8,128)(2,1)S(1)}, bf16[2,2,4,64,128]{4,3,2,1,0:T(8,128)(2,1)S(1)}) custom-call(s32[1]{0:T(128)} %bitcast.at, bf16[128,2048]{1,0:T(8,128)(2,1)} %bitcast.10, bf16[128,512]{1,0:T(8,128)(2,1)} %bitcast.13, bf16[128,512]{1,0:T(8,128)(2,1)} %bitcast.14, ...), custom_call_target="tpu_custom_call" | custom-call | bytes 4194304 | tf_op jit(solution)/shard_map/pallas_call | solution.py:307
  2.8 1.9 %collective-permute-start = (bf16[21,128,128]{2,1,0:T(8,128)(2,1)S(1)}, bf16[21,128,128]{2,1,0:T(8,128)(2,1)S(1)}, u32[]{:S(2)}, u32[]{:S(2)}) collective-permute-start(bf16[21,128,128]{2,1,0:T(8,128)(2,1)S(1)} %get-tuple-element.26), channel_id=1, source_target_pairs={{0,8},{8,0},{16,24},{24,16},{1,9},{9,1},{17,25},{25,17},{2,10},{10... | collective-permute-start | bytes 2064392 | tf_op jit(solution)/shard_map/ppermute | solution.py:297
  4.7 14.6 %collective-permute-start.1 = (bf16[2,2,4,64,128]{4,3,2,1,0:T(8,128)(2,1)S(1)}, bf16[2,2,4,64,128]{4,3,2,1,0:T(8,128)(2,1)S(1)}, u32[]{:S(2)}, u32[]{:S(2)}) collective-permute-start(bf16[2,2,4,64,128]{4,3,2,1,0:T(8,128)(2,1)S(1)} %get-tuple-element.28), channel_id=1, source_target_pairs={{0,16},{8,24},{16,0},{24,8},{1,17},{9,25},{17,1},{25,9},{2,18},{10... | collective-permute-start | bytes 786440 | tf_op jit(solution)/shard_map/ppermute | solution.py:297
  19.3 7.1 %collective-permute-done.1.far = bf16[2,2,4,64,128]{4,3,2,1,0:T(8,128)(2,1)S(1)} collective-permute-done((bf16[2,2,4,64,128]{4,3,2,1,0:T(8,128)(2,1)S(1)}, bf16[2,2,4,64,128]{4,3,2,1,0:T(8,128)(2,1)S(1)}, u32[]{:S(2)}, u32[]{:S(2)}) %collective-permute-start.1) | collective-permute-done | bytes 262176 | tf_op jit(solution)/shard_map/ppermute | solution.py:297
  26.4 1.9 %collective-permute-start.2 = (bf16[2,4,64,128]{3,2,1,0:T(8,128)(2,1)S(1)}, bf16[2,4,64,128]{3,2,1,0:T(8,128)(2,1)S(1)}, u32[]{:S(2)}, u32[]{:S(2)}) collective-permute-start(bf16[2,4,64,128]{3,2,1,0:T(8,128)(2,1)S(1)} %shard_map.138), channel_id=1, source_target_pairs={{0,8},{8,0},{16,24},{24,16},{1,9},{9,1},{17,25},{25,17},{2,10},{10... | collective-permute-start | bytes 393224 | tf_op jit(solution)/shard_map/ppermute | solution.py:297
  28.3 0.0 collective-permute-done.recv
  28.3 2.7 %shard_map.137 = (f32[8,256,128]{2,1,0:T(8,128)S(1)}, f32[4,256,128]{2,1,0:T(8,128)S(1)}, f32[4,128]{1,0:T(4,128)S(1)}, bf16[5,128,128]{2,1,0:T(8,128)(2,1)S(1)}) custom-call(s32[1]{0:T(128)} %bitcast.at, bf16[21,128,128]{2,1,0:T(8,128)(2,1)S(1)} %get-tuple-element.25.own, bf16[21,128,128]{2,1,0:T(8,128)(2,1)S(1)} %collective-permute-done.recv), custom_call_target="tpu_custom_call" | custom-call | flops 700000000 | bytes 3145728 | tf_op jit(solution)/shard_map/pallas_call | solution.py:319
  31.0 0.0 collective-permute-done.2.cross
  31.0 2.7 %shard_map.140 = (bf16[8,128,128]{2,1,0:T(8,128)(2,1)S(1)}, bf16[8,128,128]{2,1,0:T(8,128)(2,1)S(1)}, f32[512,128]{1,0:T(8,128)S(1)}, f32[8,16,128]{2,1,0:T(8,128)S(1)}) custom-call(s32[1]{0:T(128)} %bitcast.at, bf16[21,128,128]{2,1,0:T(8,128)(2,1)S(1)} %get-tuple-element.25.own, bf16[21,128,128]{2,1,0:T(8,128)(2,1)S(1)} %collective-permute-done.recv, ...), custom_call_target="tpu_custom_call" | custom-call | flops 700000000 | bytes 4194304 | tf_op jit(solution)/shard_map/pallas_call | solution.py:337
  33.8 13.1 %collective-permute-start.4 = (f32[512,128]{1,0:T(8,128)S(1)}, f32[512,128]{1,0:T(8,128)S(1)}, u32[]{:S(2)}, u32[]{:S(2)}) collective-permute-start(f32[512,128]{1,0:T(8,128)S(1)} %get-tuple-element.32), channel_id=1, source_target_pairs={{0,16},{8,24},{16,0},{24,8},{1,17},{9,25},{17,1},{25,9},{2,18},{10... | collective-permute-start | bytes 786440 | tf_op jit(solution)/shard_map/ppermute | solution.py:297
  46.9 1.9 %collective-permute-start.3 = (bf16[5,128,128]{2,1,0:T(8,128)(2,1)S(1)}, bf16[5,128,128]{2,1,0:T(8,128)(2,1)S(1)}, u32[]{:S(2)}, u32[]{:S(2)}) collective-permute-start(bf16[5,128,128]{2,1,0:T(8,128)(2,1)S(1)} %get-tuple-element.29), channel_id=1, source_target_pairs={{0,16},{8,24},{1,17},{9,25},{2,18},{10,26},{3,19},{11,27},{4,20},{... | collective-permute-start | bytes 491528 | tf_op jit(solution)/shard_map/ppermute | solution.py:327
  48.8 13.4 %collective-permute-done.3.q_late = bf16[5,128,128]{2,1,0:T(8,128)(2,1)S(1)} collective-permute-done((bf16[5,128,128]{2,1,0:T(8,128)(2,1)S(1)}, bf16[5,128,128]{2,1,0:T(8,128)(2,1)S(1)}, u32[]{:S(2)}, u32[]{:S(2)}) %collective-permute-start.3) | collective-permute-done | bytes 163872 | tf_op jit(solution)/shard_map/ppermute | solution.py:327
  62.2 0.8 shard_map.139.extra
  63.0 0.0 collective-permute-done.4.r
  63.0 0.1 shard_map.141
  63.1 2.4 %collective-permute-start.5 = (bf16[12,128,128]{2,1,0:T(8,128)(2,1)S(1)}, bf16[12,128,128]{2,1,0:T(8,128)(2,1)S(1)}, u32[]{:S(2)}, u32[]{:S(2)}) collective-permute-start(bf16[12,128,128]{2,1,0:T(8,128)(2,1)S(1)} %get-tuple-element.35), channel_id=1, source_target_pairs={{32,0},{40,8},{48,16},{56,24},{64,32},{72,40},{80,48},{88,56},{96,... | collective-permute-start | bytes 1179656 | tf_op jit(solution)/shard_map/ppermute | solution.py:333
  65.5 8.5 %collective-permute-start.6 = (bf16[12,128,128]{2,1,0:T(8,128)(2,1)S(1)}, bf16[12,128,128]{2,1,0:T(8,128)(2,1)S(1)}, u32[]{:S(2)}, u32[]{:S(2)}) collective-permute-start(bf16[12,128,128]{2,1,0:T(8,128)(2,1)S(1)} %get-tuple-element.36), channel_id=1, source_target_pairs={{32,8},{40,0},{48,24},{56,16},{64,40},{72,32},{80,56},{88,48},{96,... | collective-permute-start | bytes 1179656 | tf_op jit(solution)/shard_map/ppermute | solution.py:333
  74.0 15.3 %all_to_all.5.parts = f32[8,16,128]{2,1,0:T(8,128)S(1)} all-to-all(f32[8,16,128]{2,1,0:T(8,128)S(1)} %get-tuple-element.40), channel_id=1, replica_groups=mesh['section'=32,'ctx'=4,'dp'=8] {'dp'}, dimensions={0} | all-to-all | bytes 131072 | tf_op jit(solution)/shard_map/all_to_all | solution.py:349
  89.3 1.9 %collective-permute-start.7 = (f32[16,128]{1,0:T(8,128)S(1)}, f32[16,128]{1,0:T(8,128)S(1)}, u32[]{:S(2)}, u32[]{:S(2)}) collective-permute-start(f32[16,128]{1,0:T(8,128)S(1)} %shard_map.143.same), channel_id=1, source_target_pairs={{0,8},{8,0},{16,24},{24,16},{1,9},{9,1},{17,25},{25,17},{2,10},{10... | collective-permute-start | bytes 24584 | tf_op jit(solution)/shard_map/ppermute | solution.py:297
  91.2 1.1 %collective-permute-done.7.other = f32[16,128]{1,0:T(8,128)S(1)} collective-permute-done((f32[16,128]{1,0:T(8,128)S(1)}, f32[16,128]{1,0:T(8,128)S(1)}, u32[]{:S(2)}, u32[]{:S(2)}) %collective-permute-start.7) | collective-permute-done | bytes 8224 | tf_op jit(solution)/shard_map/ppermute | solution.py:297
  92.4 8.3 %collective-permute-start.8 = (f32[2,16,128]{2,1,0:T(8,128)S(1)}, f32[2,16,128]{2,1,0:T(8,128)S(1)}, u32[]{:S(2)}, u32[]{:S(2)}) collective-permute-start(f32[2,16,128]{2,1,0:T(8,128)S(1)} %shard_map.144.chip), channel_id=1, source_target_pairs={{0,16},{8,24},{16,0},{24,8},{1,17},{9,25},{17,1},{25,9},{2,18},{10... | collective-permute-start | bytes 49160 | tf_op jit(solution)/shard_map/ppermute | solution.py:297
  100.7 1.7 %collective-permute-done.8.far = f32[2,16,128]{2,1,0:T(8,128)S(1)} collective-permute-done((f32[2,16,128]{2,1,0:T(8,128)S(1)}, f32[2,16,128]{2,1,0:T(8,128)S(1)}, u32[]{:S(2)}, u32[]{:S(2)}) %collective-permute-start.8) | collective-permute-done | bytes 16416 | tf_op jit(solution)/shard_map/ppermute | solution.py:297
  102.4 0.6 shard_map.145
  103.0 0.0 collective-permute-done.5.same
  103.0 0.0 collective-permute-done.6.other
  103.0 1.0 shard_map.142
  (3 shorter events, 0.0 us)
Async XLA Ops:
  2.8 25.5 %collective-permute-start = (bf16[21,128,128]{2,1,0:T(8,128)(2,1)S(1)}, bf16[21,128,128]{2,1,0:T(8,128)(2,1)S(1)}, u32[]{:S(2)}, u32[]{:S(2)}) collective-permute-start(bf16[21,128,128]{2,1,0:T(8,128)(2,1)S(1)} %get-tuple-element.26), channel_id=1, source_target_pairs={{0,8},{8,0},{16,24},{24,16},{1,9},{9,1},{17,25},{25,17},{2,10},{10... | collective-permute-start | bytes 2064392 | tf_op jit(solution)/shard_map/ppermute | solution.py:297
  4.7 21.6 %collective-permute-start.1 = (bf16[2,2,4,64,128]{4,3,2,1,0:T(8,128)(2,1)S(1)}, bf16[2,2,4,64,128]{4,3,2,1,0:T(8,128)(2,1)S(1)}, u32[]{:S(2)}, u32[]{:S(2)}) collective-permute-start(bf16[2,2,4,64,128]{4,3,2,1,0:T(8,128)(2,1)S(1)} %get-tuple-element.28), channel_id=1, source_target_pairs={{0,16},{8,24},{16,0},{24,8},{1,17},{9,25},{17,1},{25,9},{2,18},{10... | collective-permute-start | bytes 786440 | tf_op jit(solution)/shard_map/ppermute | solution.py:297
  26.4 4.6 %collective-permute-start.2 = (bf16[2,4,64,128]{3,2,1,0:T(8,128)(2,1)S(1)}, bf16[2,4,64,128]{3,2,1,0:T(8,128)(2,1)S(1)}, u32[]{:S(2)}, u32[]{:S(2)}) collective-permute-start(bf16[2,4,64,128]{3,2,1,0:T(8,128)(2,1)S(1)} %shard_map.138), channel_id=1, source_target_pairs={{0,8},{8,0},{16,24},{24,16},{1,9},{9,1},{17,25},{25,17},{2,10},{10... | collective-permute-start | bytes 393224 | tf_op jit(solution)/shard_map/ppermute | solution.py:297
  33.8 29.2 %collective-permute-start.4 = (f32[512,128]{1,0:T(8,128)S(1)}, f32[512,128]{1,0:T(8,128)S(1)}, u32[]{:S(2)}, u32[]{:S(2)}) collective-permute-start(f32[512,128]{1,0:T(8,128)S(1)} %get-tuple-element.32), channel_id=1, source_target_pairs={{0,16},{8,24},{16,0},{24,8},{1,17},{9,25},{17,1},{25,9},{2,18},{10... | collective-permute-start | bytes 786440 | tf_op jit(solution)/shard_map/ppermute | solution.py:297
  46.9 15.3 %collective-permute-start.3 = (bf16[5,128,128]{2,1,0:T(8,128)(2,1)S(1)}, bf16[5,128,128]{2,1,0:T(8,128)(2,1)S(1)}, u32[]{:S(2)}, u32[]{:S(2)}) collective-permute-start(bf16[5,128,128]{2,1,0:T(8,128)(2,1)S(1)} %get-tuple-element.29), channel_id=1, source_target_pairs={{0,16},{8,24},{1,17},{9,25},{2,18},{10,26},{3,19},{11,27},{4,20},{... | collective-permute-start | bytes 491528 | tf_op jit(solution)/shard_map/ppermute | solution.py:327
  63.1 39.9 %collective-permute-start.5 = (bf16[12,128,128]{2,1,0:T(8,128)(2,1)S(1)}, bf16[12,128,128]{2,1,0:T(8,128)(2,1)S(1)}, u32[]{:S(2)}, u32[]{:S(2)}) collective-permute-start(bf16[12,128,128]{2,1,0:T(8,128)(2,1)S(1)} %get-tuple-element.35), channel_id=1, source_target_pairs={{32,0},{40,8},{48,16},{56,24},{64,32},{72,40},{80,48},{88,56},{96,... | collective-permute-start | bytes 1179656 | tf_op jit(solution)/shard_map/ppermute | solution.py:333
  65.5 37.5 %collective-permute-start.6 = (bf16[12,128,128]{2,1,0:T(8,128)(2,1)S(1)}, bf16[12,128,128]{2,1,0:T(8,128)(2,1)S(1)}, u32[]{:S(2)}, u32[]{:S(2)}) collective-permute-start(bf16[12,128,128]{2,1,0:T(8,128)(2,1)S(1)} %get-tuple-element.36), channel_id=1, source_target_pairs={{32,8},{40,0},{48,24},{56,16},{64,40},{72,32},{80,56},{88,48},{96,... | collective-permute-start | bytes 1179656 | tf_op jit(solution)/shard_map/ppermute | solution.py:333
  89.3 3.1 %collective-permute-start.7 = (f32[16,128]{1,0:T(8,128)S(1)}, f32[16,128]{1,0:T(8,128)S(1)}, u32[]{:S(2)}, u32[]{:S(2)}) collective-permute-start(f32[16,128]{1,0:T(8,128)S(1)} %shard_map.143.same), channel_id=1, source_target_pairs={{0,8},{8,0},{16,24},{24,16},{1,9},{9,1},{17,25},{25,17},{2,10},{10... | collective-permute-start | bytes 24584 | tf_op jit(solution)/shard_map/ppermute | solution.py:297
  92.4 10.0 %collective-permute-start.8 = (f32[2,16,128]{2,1,0:T(8,128)S(1)}, f32[2,16,128]{2,1,0:T(8,128)S(1)}, u32[]{:S(2)}, u32[]{:S(2)}) collective-permute-start(f32[2,16,128]{2,1,0:T(8,128)S(1)} %shard_map.144.chip), channel_id=1, source_target_pairs={{0,16},{8,24},{16,0},{24,8},{1,17},{9,25},{17,1},{25,9},{2,18},{10... | collective-permute-start | bytes 49160 | tf_op jit(solution)/shard_map/ppermute | solution.py:297
